TPU v7x, 512 devices: a whole 4x4x16 slice. The times are simulated.
512 devices in a mesh: mom: 8 (over y, x_lo), shard: 64 (over x_hi, z, core).
Axes of the slice: x: 4 (x_hi: 2, x_lo: 2; x = x_hi * 2 + x_lo), y: 4, z: 16, core: 2. Of those that a mesh axis runs over, the one named last changes fastest.
Arguments:
- green_ret: bfloat16 [8, 256, 8, 2, 128, 128], P('mom', 'shard'), may hold values from -4 to 4
- broadening: bfloat16 [2, 128, 128], replicated, may hold values from -0.5 to 0.5
- occupation: float32 [8, 256], P('mom', 'shard'), may hold values from 0.1 to 1
- neighbours: int32 [64, 4], replicated, may hold values from 0 to 63, as said below
- orbitals: int32 [64], replicated, may hold values from 4 to 16
- coupling: bfloat16 [64, 4, 256, 256], P('shard'), may hold values from -0.1875 to 0.1875
- phonon: float32 [8, 2, 256], replicated, may hold values from -5 to 5
- mode_table: int32 [8, 8], replicated, may hold values from 0 to 7, as said below
Outputs:
- self_energy: bfloat16 [8, 256, 64, 2, 256], P('mom', None, 'shard')
Inputs may be any that keep to these rules, and one draw needn't show every extreme that they name: `neighbours`: row a holds 4 distinct atoms of a's own layer block (atoms 8 * (a // 8) onward), none equal to a; the first is a with its lowest bit flipped. `mode_table`: each entry names one of the 8 phonon modes.
All inputs are finite; a program needn't handle non-finite values.
Results may differ from a plain program's by a relative error of at most 0.013.
Values may be sent and summed in bfloat16 or wider, within the bound.
No kernel may reach another device: no remote copies, remote signals or barrier semaphores. Data moves between devices by JAX's collectives and lax.ppermute only.
A program may use at most 192 MiB of HBM per device.

v0:
```python
import math

import jax
import jax.numpy as jnp
from jax import lax
from jax.sharding import PartitionSpec as P

NORB = 16
ATL = 8
NBR = 4
ENERGIES = 256
LAYERS = 8
PAIR = 256
ATOMS = 64


def dft_tables(length):
    counter = jnp.arange(length, dtype=jnp.int32)
    phases = counter[:, None] * counter[None, :] % length
    angles = phases.astype(jnp.float32) * (2.0 * math.pi / length)
    return (jnp.cos(angles).astype(jnp.bfloat16), jnp.sin(angles).astype(jnp.bfloat16))


def local(green_ret, broadening, occupation, neighbours, orbitals, coupling, phonon, mode_table):
    highest = lax.Precision.HIGHEST
    greens = green_ret[0]
    energy_dev = greens.shape[0]
    mixing = jnp.stack(
        [
            jnp.concatenate([broadening[0], broadening[1]], axis=1),
            jnp.concatenate([-broadening[1], broadening[0]], axis=1),
        ],
        axis=0,
    )
    left = jnp.einsum("elpik,pkq->eliq", greens, mixing, preferred_element_type=jnp.float32).astype(
        jnp.bfloat16
    )
    slot_atoms = neighbours % ATL
    selector = slot_atoms[:, :, None] == jnp.arange(ATL, dtype=jnp.int32)[None, None, :]
    layer_orbitals = jnp.repeat(orbitals.reshape(LAYERS, ATL), ATL, axis=0)
    partner_count = jnp.sum(jnp.where(selector, layer_orbitals[:, None, :], 0), axis=2)
    green_re = greens[:, :, 0]
    green_im = greens[:, :, 1]
    partner = jnp.stack(
        [
            jnp.concatenate([green_re, green_im], axis=-1),
            jnp.concatenate([-green_im, green_re], axis=-1),
        ],
        axis=2,
    )
    blocks = jnp.einsum("elik,elpjk->elpij", left, partner, preferred_element_type=jnp.float32)
    blocks = blocks.reshape(energy_dev, LAYERS, 2, ATL, NORB, ATL, NORB).transpose(
        0, 1, 3, 5, 2, 4, 6
    )
    slot_index = slot_atoms.reshape(LAYERS, ATL, NBR)
    chosen = jnp.take_along_axis(blocks, slot_index[None, :, :, :, None, None, None], axis=3)
    chosen = chosen.reshape(energy_dev, ATOMS, NBR, 2, NORB, NORB)
    counter = jnp.arange(NORB, dtype=jnp.int32)
    row_mask = counter[None, :] < orbitals[:, None]
    column_mask = counter[None, None, :] < partner_count[:, :, None]
    pair_mask = (row_mask[:, None, :, None] & column_mask[:, :, None, :]).astype(jnp.float32)
    scaled = (
        chosen * occupation[0][:, None, None, None, None, None] * pair_mask[None, :, :, None, :, :]
    )
    pair_blocks = scaled.reshape(energy_dev, ATOMS, NBR, 2, PAIR).astype(jnp.bfloat16)
    arrived = lax.all_to_all(pair_blocks, "shard", split_axis=1, concat_axis=0, tiled=True)
    atom_dev = arrived.shape[1]
    mixed_terms = jnp.einsum(
        "eanpx,anxy->eapy", arrived, coupling, preferred_element_type=jnp.float32
    )
    first_atom = lax.axis_index("shard") * atom_dev
    own_orbitals = lax.dynamic_slice_in_dim(orbitals, first_atom, atom_dev)
    pair_index = jnp.arange(PAIR, dtype=jnp.int32)
    own_mask = (
        (pair_index[None, :] // NORB < own_orbitals[:, None])
        & (pair_index[None, :] % NORB < own_orbitals[:, None])
    ).astype(jnp.float32)
    coupled = (mixed_terms * own_mask[None, :, None, :]).astype(jnp.bfloat16)
    cos_table, sin_table = dft_tables(ENERGIES)
    flat_coupled = coupled.reshape(ENERGIES, -1)
    part_cos = jnp.dot(cos_table, flat_coupled, preferred_element_type=jnp.float32).reshape(
        ENERGIES, atom_dev, 2, PAIR
    )
    part_sin = jnp.dot(sin_table, flat_coupled, preferred_element_type=jnp.float32).reshape(
        ENERGIES, atom_dev, 2, PAIR
    )
    time_data = jnp.stack(
        [part_cos[:, :, 0] + part_sin[:, :, 1], part_cos[:, :, 1] - part_sin[:, :, 0]], axis=2
    ).astype(jnp.bfloat16)
    own_momentum = lax.axis_index("mom")
    mode_count = phonon.shape[0]
    mode_ids = jnp.arange(mode_count, dtype=jnp.int32)
    own_modes = lax.dynamic_slice_in_dim(mode_table, own_momentum, 1, 0)[0]
    phonon_flat = phonon.reshape(mode_count, -1)
    received = lax.all_gather(time_data[None], "mom", axis=0, tiled=True)
    row_count = received.shape[0]
    one_hot = (own_modes[:, None] == mode_ids[None, :]).astype(jnp.float32)
    kernel = jnp.dot(one_hot, phonon_flat, precision=highest).reshape(row_count, 2, ENERGIES)
    values = received.astype(jnp.float32)
    kernel_re = kernel[:, 0][:, :, None, None]
    kernel_im = kernel[:, 1][:, :, None, None]
    add_re = jnp.sum(kernel_re * values[:, :, :, 0] - kernel_im * values[:, :, :, 1], axis=0)
    add_im = jnp.sum(kernel_re * values[:, :, :, 1] + kernel_im * values[:, :, :, 0], axis=0)
    summed = jnp.stack([add_re, add_im], axis=2)
    convolved = summed.astype(jnp.bfloat16)
    flat_conv = convolved.reshape(ENERGIES, -1)
    back_cos = jnp.dot(cos_table, flat_conv, preferred_element_type=jnp.float32).reshape(
        ENERGIES, atom_dev, 2, PAIR
    )
    back_sin = jnp.dot(sin_table, flat_conv, preferred_element_type=jnp.float32).reshape(
        ENERGIES, atom_dev, 2, PAIR
    )
    result_re = (back_cos[:, :, 0] - back_sin[:, :, 1]) * (1.0 / ENERGIES)
    result_im = (back_cos[:, :, 1] + back_sin[:, :, 0]) * (1.0 / ENERGIES)
    return jnp.stack([result_re, result_im], axis=2)[None].astype(jnp.bfloat16)


def solution(mesh):
    in_specs = (
        P("mom", "shard", None, None, None, None),
        P(),
        P("mom", "shard"),
        P(),
        P(),
        P("shard", None, None, None),
        P(),
        P(),
    )
    out_specs = P("mom", None, "shard", None, None)
    return jax.shard_map(local, mesh=mesh, in_specs=in_specs, out_specs=out_specs, check_vma=False)
```

profile of v0, /device:TPU:1, one launch (start us, length us, event | category | flops | bytes accessed | tf_op | source)
XLA Modules:
  0.0 248.5 jit_solution(2611192785870008069)
XLA Ops:
  6.5 0.0 copy-start
  6.5 1.8 copy.111
  8.3 0.0 copy-start.2
  8.3 1.1 slice_bitcast_fusion.2
  9.4 0.1 fusion.75
  9.6 0.1 reshape.372
  9.7 0.6 copy-done.1
  10.3 0.1 copy.96
  10.4 0.1 copy.95
  10.5 4.1 %maximum_bitcast_fusion = (bf16[4,8,1,128,256]{4,3,2,1,0:T(8,128)(2,1)}, bf16[4,8,1,128,256]{4,3,2,1,0:T(8,128)(2,1)}) fusion(bf16[4,8,128,128]{3,2,1,0:T(8,128)(2,1)S(1)} %get-tuple-element.9, bf16[4,8,128,128]{3,2,1,0:T(8,128)(2,1)} %get-tuple-element.10, bf16[4,8,128,128]{3,2,1,0:T(8,128)(2,1)S(1)} %fusion.75), kind=kLoop, calls=%fused_computation.9 | loop fusion | flops 8388608 | bytes 7340032 | tf_op jit(solution)/shard_map/stack | solution.py:44
  14.7 6.8 %fusion.4 = f32[4,8,2,128,128]{3,4,2,1,0:T(8,128)} fusion(bf16[4,8,1,128,256]{4,3,2,1,0:T(8,128)(2,1)} %get-tuple-element.16, bf16[4,8,1,128,256]{4,3,2,1,0:T(8,128)(2,1)} %get-tuple-element.15, bf16[1,4,8,2,128,128]{5,4,3,2,1,0:T(8,128)(2,1)} %param.8, bf16[1,128,256]{1,2,0:T(8,128)(2,1)S(1)} %get-tuple-element.20, ...), kind=kOutput, calls=%fused_computation.6 | convolution fusion | flops 1077149696 | bytes 10616832 | tf_op jit(solution)/shard_map/elik,elpjk->elpij/dot_general | solution.py:51
  21.5 19.6 %reshape.371 = f32[4,8,2,8,16,8,16]{4,3,6,5,2,1,0:T(8,128)} reshape(f32[4,8,2,128,128]{3,4,2,1,0:T(8,128)} %fusion.4) | data formatting | bytes 8388608 | tf_op jit(solution)/shard_map/reshape | solution.py:52
  41.1 33.9 %copy.72 = f32[4,8,2,8,16,8,16]{6,4,2,5,3,1,0:T(8,128)} copy(f32[4,8,2,8,16,8,16]{4,3,6,5,2,1,0:T(8,128)} %reshape.371) | data formatting | bytes 8388608 | tf_op jit(solution)/shard_map/reshape | solution.py:52
  74.9 0.0 copy-done.3
  74.9 0.1 copy.94
  75.0 0.1 reshape.378
  75.1 14.9 %gather_fusion = f32[256,4,2,16,16]{4,3,2,1,0:T(8,128)} fusion(f32[4,8,8,8,2,16,16]{6,5,4,3,2,1,0:T(8,128)} %bitcast.180, s32[256]{0:T(256)S(1)} %reshape.378), kind=kCustom, calls=%fused_computation | custom fusion | bytes 4197376 | tf_op jit(solution)/shard_map/jit(take_along_axis)/gather | solution.py:56
  90.1 12.3 %reshape.392 = f32[4,64,4,2,256]{4,3,0,2,1:T(2,128)S(1)} reshape(f32[4,8,8,4,2,16,16]{6,5,4,0,3,2,1:T(8,128)} %bitcast.181) | data formatting | bytes 4194304 | tf_op jit(solution)/shard_map/jit(take_along_axis)/gather | solution.py:56
  102.4 0.1 copy.77
  102.5 0.1 broadcast_in_dim.26
  102.6 0.1 broadcast_in_dim.27
  102.8 0.2 copy.78
  103.0 0.1 copy.65
  103.1 1.6 fusion.10
  104.7 19.6 %all-to-all-start = ((bf16[4,64,4,2,256]{4,0,2,3,1:T(4,128)(2,1)}), bf16[4,64,4,2,256]{4,0,2,3,1:T(4,128)(2,1)S(1)}, u32[]{:S(2)}, u32[]{:S(2)}) async-start(bf16[4,64,4,2,256]{4,0,2,3,1:T(4,128)(2,1)} %fusion.10), calls=%async_computation | async-start | bytes 2097152 | tf_op jit(solution)/shard_map/all_to_all | solution.py:66
  124.3 0.0 all-gather.2.cloned.1.call-start
  124.4 0.6 dynamic_slice.7
  125.0 0.6 and_convert_fusion
  125.6 50.5 %all-to-all-done = bf16[4,64,4,2,256]{4,0,2,3,1:T(4,128)(2,1)S(1)} async-done(((bf16[4,64,4,2,256]{4,0,2,3,1:T(4,128)(2,1)}), bf16[4,64,4,2,256]{4,0,2,3,1:T(4,128)(2,1)S(1)}, u32[]{:S(2)}, u32[]{:S(2)}) %all-to-all-start) | async-done | bytes 1048608 | tf_op jit(solution)/shard_map/all_to_all | solution.py:66
  176.1 0.4 copy.79
  176.5 0.5 reshape.373
  177.0 0.5 fusion.18
  177.5 0.0 copy-start.5
  177.5 1.1 convolution_bitcast_fusion.2
  178.6 1.1 convolution_bitcast_fusion.3
  179.7 0.1 fusion.37
  179.8 0.7 pad_maximum_fusion
  180.6 0.0 all-gather.2.cloned.1.call-update
  180.6 0.7 dynamic-slice_bitcast_fusion
  181.3 0.2 fusion.51
  181.5 53.8 %all-gather.2.cloned.1.call-done = bf16[8,256,1,2,256]{4,1,3,2,0:T(8,128)(2,1)} async-done(((bf16[1,256,1,2,256]{4,1,3,2,0:T(8,128)(2,1)}), bf16[8,256,1,2,256]{4,1,3,2,0:T(8,128)(2,1)}) %all-gather.2.cloned.1.call-update) | async-done | bytes 2097168 | tf_op jit(solution)/shard_map/all_gather | solution.py:95
  235.3 2.0 convert_element_type.93
  237.3 0.8 subtract_reduce_fusion
  238.1 0.1 copy.82
  238.3 1.1 convolution_bitcast_fusion
  239.4 1.1 convolution_bitcast_fusion.1
  240.5 0.1 fusion.27
  240.6 1.0 copy.83
  (20 shorter events, 0.2 us)
Async XLA Ops:
  6.5 170.4 %copy-start = (bf16[1,4,256,256]{3,2,1,0:T(8,128)(2,1)S(1)}, bf16[1,4,256,256]{3,2,1,0:T(8,128)(2,1)}, u32[]{:S(2)}) copy-start(bf16[1,4,256,256]{3,2,1,0:T(8,128)(2,1)} %param.13) | copy-start | bytes 1572868
  8.3 1.3 copy-start.2
  9.4 0.8 copy-start.1
  41.1 33.9 %copy-start.3 = (s32[64,4]{0,1:T(4,128)S(1)}, s32[64,4]{0,1:T(4,128)}, u32[]{:S(2)}) copy-start(s32[64,4]{0,1:T(4,128)} %param.11) | copy-start | bytes 3076
  90.1 13.0 %copy-start.4 = (f32[1,4]{1,0:T(1,128)S(1)}, f32[1,4]{1,0:T(1,128)}, u32[]{:S(2)}) copy-start(f32[1,4]{1,0:T(1,128)} %param.10) | copy-start | bytes 52
  104.7 71.4 %all-to-all-start = ((bf16[4,64,4,2,256]{4,0,2,3,1:T(4,128)(2,1)}), bf16[4,64,4,2,256]{4,0,2,3,1:T(4,128)(2,1)S(1)}, u32[]{:S(2)}, u32[]{:S(2)}) async-start(bf16[4,64,4,2,256]{4,0,2,3,1:T(4,128)(2,1)} %fusion.10), calls=%async_computation | async-start | bytes 2097152 | tf_op jit(solution)/shard_map/all_to_all | solution.py:66
  124.3 110.9 %all-gather.2.cloned.1.call-start = ((), (), s32[]{:S(2)}) async-start(), calls=%async_computation.1 | async-start | bytes 2359296 | tf_op jit(solution)/shard_map/all_gather | solution.py:95
  177.5 3.8 %copy-start.5 = (f32[8,2,256]{2,1,0:T(2,128)S(1)}, f32[8,2,256]{2,1,0:T(2,128)}, u32[]{:S(2)}) copy-start(f32[8,2,256]{2,1,0:T(2,128)} %param.14) | copy-start | bytes 49156
Sparse Core Ops, SparseCore 0:
  180.7 54.5 all-gather.1
where the time goes:
time: 250 us; the launch traced here: 248 us
  waiting for transfers between devices  104 us (42%)
  local copies, waits for them, and re-layouts  88.6 us (35%)
  starting transfers between devices  19.6 us (8%)
  between operations  13.6 us (5%)
  matrix products  11.9 us (5%)
  other arithmetic  10.5 us (4%)
    all_gather x1, waiting for transfers between devices, local(): received = lax.all_gather(time_data[None], 'mom', axis=0, tiled=True)  53.8 us
    reshape x2, local copies, waits for them, and re-layouts, local(): blocks.reshape(energy_dev, LAYERS, 2, ATL, NORB, ATL, NORB)  53.4 us
    all_to_all x1, waiting for transfers between devices, local(): lax.all_to_all(pair_blocks, 'shard', split_axis=1, concat_axis=0, tiled=T...  50.5 us
    gather x3, local copies, waits for them, and re-layouts, local(): jnp.take_along_axis(blocks, slot_index[None, :, :, :, None, None, None],...  27.4 us
    all_to_all x1, starting transfers between devices, local(): lax.all_to_all(pair_blocks, 'shard', split_axis=1, concat_axis=0, tiled=T...  19.6 us
    dot_general x1, matrix products, local(): jnp.einsum('elik,elpjk->elpij', left, partner, preferred_element_type=jnp...  6.77 us
  transfers between devices with their start and end apart: 2, of which 2 were waited for; matrix products, arithmetic and copies ran while one was open for 1% of the time, Pallas kernels for 0%

commit v1 on v0

v1 whole, which is shorter than its diff:
```python
import functools

import jax
import jax.numpy as jnp
import numpy as np
from jax import lax
from jax.experimental import pallas as pl
from jax.experimental.pallas import tpu as pltpu
from jax.sharding import PartitionSpec as P

NORB = 16
ATL = 8
NBR = 4
ENERGIES = 256
LAYERS = 8
ORB = 128
PAIR = 256
ATOMS = 64
KPTS = 8
CHUNKS = 1

F32 = jnp.float32
BF16 = jnp.bfloat16
VMEM_SPEC = pl.BlockSpec(memory_space=pltpu.VMEM)


def dft_tables(length):
    counter = np.arange(length)
    angles = (counter[:, None] * counter[None, :] % length) * (2.0 * np.pi / length)
    return np.cos(angles).astype(jnp.bfloat16), np.sin(angles).astype(jnp.bfloat16)


def pairs_kernel(first, occ_ref, nbr_ref, orb_ref, green_ref, mix_ref, out_ref):
    layer = pl.program_id(0)
    energies = green_ref.shape[1]
    rows = []
    for e in range(energies):
        rows.append(jnp.concatenate([green_ref[0, e, 0, 0], green_ref[0, e, 0, 1]], axis=1))
    left = jnp.dot(jnp.concatenate(rows, axis=0), mix_ref[...], preferred_element_type=F32)
    left = left.astype(BF16)
    full = []
    for e in range(energies):
        green_re = green_ref[0, e, 0, 0]
        green_im = green_ref[0, e, 0, 1]
        partner = jnp.concatenate(
            [
                jnp.concatenate([green_re, green_im], axis=1),
                jnp.concatenate([-green_im, green_re], axis=1),
            ],
            axis=0,
        )
        block = lax.dot_general(
            left[e * ORB : (e + 1) * ORB],
            partner,
            (((1,), (1,)), ((), ())),
            preferred_element_type=F32,
        )
        full.append((block * occ_ref[0, first + e]).astype(BF16))
    lane = lax.broadcasted_iota(jnp.int32, (1, ORB), 1)
    slot = (lane // NORB) % NBR
    column = lane % NORB
    source = lax.broadcasted_iota(jnp.int32, (ORB, ORB), 0)
    row = lax.broadcasted_iota(jnp.int32, (energies * NORB, ORB), 0) % NORB
    low = lax.broadcasted_iota(jnp.int32, (energies * NORB, ORB), 1) < ORB // 2
    for a in range(ATL):
        atom = layer * ATL + a
        target = jnp.full((1, ORB), -1, jnp.int32)
        for n in range(NBR):
            partner_atom = nbr_ref[atom, n]
            start = (partner_atom % ATL) * NORB
            chosen = (slot == n) & (column < orb_ref[partner_atom])
            target = jnp.where(chosen, start + column, target)
        select = jnp.where(source == target, 1.0, 0.0).astype(BF16)
        part_rows = [
            full[e][a * NORB : (a + 1) * NORB, p * ORB : (p + 1) * ORB]
            for p in range(2)
            for e in range(energies)
        ]
        picked = jnp.dot(jnp.concatenate(part_rows, axis=0), select, preferred_element_type=F32)
        half = energies * NORB
        merged = jnp.where(low, picked[:half], picked[half:])
        merged = jnp.where(row < orb_ref[atom], merged, 0.0).astype(BF16)
        out_ref[a] = merged.reshape(energies, NORB, ORB)


def make_pairs(green_ret, mixing, occupation, neighbours, orbitals, chunk):
    energies = green_ret.shape[1] // CHUNKS
    smem = pl.BlockSpec(memory_space=pltpu.SMEM)
    return pl.pallas_call(
        functools.partial(pairs_kernel, chunk * energies),
        grid=(LAYERS,),
        in_specs=[
            smem,
            smem,
            smem,
            pl.BlockSpec((1, energies, 1, 2, ORB, ORB), lambda l: (0, chunk, l, 0, 0, 0)),
            pl.BlockSpec((2 * ORB, 2 * ORB), lambda l: (0, 0)),
        ],
        out_specs=pl.BlockSpec((ATL, energies, NORB, ORB), lambda l: (l, 0, 0, 0)),
        out_shape=jax.ShapeDtypeStruct((ATOMS, energies, NORB, ORB), BF16),
        name=f"pairs{chunk}",
    )(occupation, neighbours, orbitals, green_ret, mixing)


def couple_kernel(*refs):
    arrived, (weight_ref, mask_ref, table_ref, out_ref, wide) = refs[:CHUNKS], refs[CHUNKS:]
    per_chunk = arrived[0].shape[1]
    for chunk in range(CHUNKS):
        rows = arrived[chunk].shape[0] * per_chunk * NORB
        wide[chunk * rows : (chunk + 1) * rows] = (
            arrived[chunk][...].reshape(rows, ORB).astype(F32)
        )
    total = jnp.zeros((ENERGIES, 2 * PAIR), F32)
    for step in range(NORB // 2):
        rows = jnp.concatenate(
            [wide[pl.ds(2 * step + u, ENERGIES, stride=NORB), :].astype(BF16) for u in range(2)],
            axis=1,
        )
        total = total + jnp.dot(rows, weight_ref[step], preferred_element_type=F32)
    coupled = (total * mask_ref[...]).astype(BF16)
    spectra = jnp.dot(table_ref[...], coupled, preferred_element_type=F32)
    out_ref[:, :PAIR] = (spectra[:ENERGIES, :PAIR] + spectra[ENERGIES:, PAIR:]).astype(BF16)
    out_ref[:, PAIR:] = (spectra[:ENERGIES, PAIR:] - spectra[ENERGIES:, :PAIR]).astype(BF16)


def convolve_kernel(values_ref, kernel_ref, out_ref):
    for target in range(KPTS):
        sum_re = 0.0
        sum_im = 0.0
        for source in range(KPTS):
            column = (target * KPTS + source) * 2
            kernel_re = kernel_ref[:, column : column + 1]
            kernel_im = kernel_ref[:, column + 1 : column + 2]
            value_re = values_ref[source, :, :PAIR].astype(F32)
            value_im = values_ref[source, :, PAIR:].astype(F32)
            sum_re = sum_re + (kernel_re * value_re - kernel_im * value_im)
            sum_im = sum_im + (kernel_re * value_im + kernel_im * value_re)
        out_ref[target, :, :PAIR] = sum_re.astype(BF16)
        out_ref[target, :, PAIR:] = sum_im.astype(BF16)


def back_kernel(values_ref, table_ref, out_ref):
    values = jnp.concatenate([values_ref[:, :PAIR], values_ref[:, PAIR:]], axis=0)
    result = jnp.dot(table_ref[...], values, preferred_element_type=F32)
    out_ref[...] = (result * (1.0 / ENERGIES)).astype(BF16)


def local(
    green_ret, broadening, occupation, neighbours, orbitals, coupling, phonon, mode_table
):
    highest = lax.Precision.HIGHEST
    mixing = jnp.concatenate(
        [
            jnp.concatenate([broadening[0], broadening[1]], axis=1),
            jnp.concatenate([-broadening[1], broadening[0]], axis=1),
        ],
        axis=0,
    )
    arrived = []
    for chunk in range(CHUNKS):
        pairs = make_pairs(green_ret, mixing, occupation, neighbours, orbitals, chunk)
        arrived.append(lax.all_to_all(pairs, "shard", split_axis=0, concat_axis=0, tiled=True))

    parts = coupling.reshape(NBR, NORB, NORB, PAIR).transpose(1, 0, 2, 3)
    parts = parts.reshape(NORB, NBR * NORB, PAIR)
    zeros = jnp.zeros_like(parts)
    weights = jnp.concatenate(
        [
            jnp.concatenate([parts, zeros], axis=2),
            jnp.concatenate([zeros, parts], axis=2),
        ],
        axis=1,
    ).reshape(NORB // 2, 4 * NBR * NORB, 2 * PAIR)
    own_atom = lax.axis_index("shard")
    own_count = lax.dynamic_slice_in_dim(orbitals, own_atom, 1)[0]
    pair_index = jnp.arange(2 * PAIR, dtype=jnp.int32) % PAIR
    own_mask = (pair_index // NORB < own_count) & (pair_index % NORB < own_count)
    own_mask = own_mask.astype(F32)[None, :]
    cos_table, sin_table = dft_tables(ENERGIES)
    forward = jnp.asarray(np.concatenate([cos_table, sin_table], axis=0))
    timed = pl.pallas_call(
        couple_kernel,
        in_specs=[VMEM_SPEC] * (CHUNKS + 3),
        out_specs=VMEM_SPEC,
        out_shape=jax.ShapeDtypeStruct((ENERGIES, 2 * PAIR), BF16),
        scratch_shapes=[pltpu.VMEM((ENERGIES * NORB, ORB), F32)],
        name="couple",
    )(*arrived, weights, own_mask, forward)

    span = ENERGIES // KPTS
    own_momentum = lax.axis_index("mom")
    own_phonon = lax.dynamic_slice_in_dim(phonon, own_momentum * span, span, 2)
    mode_ids = jnp.arange(phonon.shape[0], dtype=jnp.int32)
    one_hot = (mode_table.reshape(-1, 1) == mode_ids[None, :]).astype(F32)
    kernel = jnp.dot(one_hot, own_phonon.reshape(phonon.shape[0], -1), precision=highest)
    kernel = kernel.reshape(KPTS * KPTS * 2, span).T

    moved = lax.all_to_all(
        timed.reshape(KPTS, span, 2 * PAIR), "mom", split_axis=0, concat_axis=0, tiled=True
    )
    convolved = pl.pallas_call(
        convolve_kernel,
        in_specs=[VMEM_SPEC] * 2,
        out_specs=VMEM_SPEC,
        out_shape=jax.ShapeDtypeStruct((KPTS, span, 2 * PAIR), BF16),
        name="convolve",
    )(moved, kernel)
    returned = lax.all_to_all(convolved, "mom", split_axis=0, concat_axis=0, tiled=True)

    wide_cos = cos_table.astype(np.float32)
    wide_sin = sin_table.astype(np.float32)
    backward = np.stack(
        [
            np.concatenate([wide_cos, -wide_sin], axis=1),
            np.concatenate([wide_sin, wide_cos], axis=1),
        ],
        axis=1,
    ).reshape(2 * ENERGIES, 2 * ENERGIES)
    result = pl.pallas_call(
        back_kernel,
        in_specs=[VMEM_SPEC] * 2,
        out_specs=VMEM_SPEC,
        out_shape=jax.ShapeDtypeStruct((2 * ENERGIES, PAIR), BF16),
        name="back",
    )(returned.reshape(ENERGIES, 2 * PAIR), jnp.asarray(backward, dtype=BF16))
    return result.reshape(1, ENERGIES, 1, 2, PAIR)


def solution(mesh):
    in_specs = (
        P("mom", "shard", None, None, None, None),
        P(),
        P("mom", "shard"),
        P(),
        P(),
        P("shard", None, None, None),
        P(),
        P(),
    )
    out_specs = P("mom", None, "shard", None, None)
    return jax.shard_map(local, mesh=mesh, in_specs=in_specs, out_specs=out_specs, check_vma=False)
```

time: 250 us -> 121 us (0.48)
  the two profiles are of different devices: /device:TPU:1 before, /device:TPU:64 now
where the time goes in v1:
time: 121 us; the launch traced here: 120 us
  waiting for transfers between devices  57.5 us (48%)
  starting transfers between devices  22.4 us (19%)
  Pallas kernels  17 us (14%)
  blocking collectives  11.3 us (9%)
  local copies, waits for them, and re-layouts  7.26 us (6%)
  other arithmetic  4.22 us (3%)
    all_to_all x1, waiting for transfers between devices, local(): lax.all_to_all(pairs, 'shard', split_axis=0, concat_axis=0, tiled=True)  51.2 us
    all_to_all x1, starting transfers between devices, local(): lax.all_to_all(pairs, 'shard', split_axis=0, concat_axis=0, tiled=True)  17.9 us
    all_to_all x1, blocking collectives, local(): lax.all_to_all(convolved, 'mom', split_axis=0, concat_axis=0, tiled=True)  11.3 us
    pallas_call x1, Pallas kernels, make_pairs(): pl.pallas_call(functools.partial(pairs_kernel, chunk * energies), grid=(L...  8.37 us
    all_to_all x1, waiting for transfers between devices, local(): lax.all_to_all(timed.reshape(KPTS, span, 2 * PAIR), 'mom', split_axis=0,...  6.25 us
    all_to_all x1, starting transfers between devices, local(): lax.all_to_all(timed.reshape(KPTS, span, 2 * PAIR), 'mom', split_axis=0,...  4.5 us
    pallas_call x1, Pallas kernels, local(): pl.pallas_call(couple_kernel, in_specs=[VMEM_SPEC] * (CHUNKS + 3), out_sp...  3.83 us
    unnamed x13, local copies, waits for them, and re-layouts  3.09 us
  transfers between devices with their start and end apart: 2, of which 2 were waited for; matrix products, arithmetic and copies ran while one was open for 4% of the time, Pallas kernels for 0%

profile of v1, /device:TPU:64, one launch (start us, length us, event | category | flops | bytes accessed | tf_op | source)
XLA Modules:
  0.0 119.9 jit_solution(6443203314521610708)
XLA Ops:
  0.0 0.0 copy-start
  0.0 0.8 slice_bitcast_fusion
  0.8 0.8 fusion.5
  1.6 1.4 %copy.14.nbr_ref = s32[64,4]{1,0:T(8,128)} copy(s32[64,4]{0,1:T(4,128)} %param.13) | data formatting | bytes 2048 | tf_op args[3]
  2.9 0.7 maximum_maximum_fusion.mix_ref
  3.6 0.0 copy-start.3
  3.6 8.4 %pairs0.1 = bf16[64,4,16,128]{3,2,1,0:T(8,128)(2,1)} custom-call(f32[1,4]{1,0:T(1,128)} %occ_ref.1, s32[64,4]{1,0:T(8,128)} %copy.14.nbr_ref, s32[64]{0:T(128)} %orb_ref.1, bf16[1,4,8,2,128,128]{5,4,3,2,1,0:T(8,128)(2,1)} %green_ref.1, bf16[256,256]{1,0:T(8,128)(2,1)} %maximum_maximum_fusion.mix_ref), custom_call_target="tpu_custom_call" | custom-call | tf_op jit(solution)/shard_map/pairs0/pallas_call | solution.py:89
  12.0 0.0 copy-start.5
  12.0 17.9 %all-to-all-start = ((bf16[64,4,16,128]{3,2,1,0:T(8,128)(2,1)}), bf16[64,4,16,128]{3,2,1,0:T(8,128)(2,1)S(1)}, u32[]{:S(2)}, u32[]{:S(2)}) async-start(bf16[64,4,16,128]{3,2,1,0:T(8,128)(2,1)} %pairs0.1), calls=%async_computation | async-start | bytes 2097152 | tf_op jit(solution)/shard_map/all_to_all | solution.py:162
  29.9 0.0 copy-done.3
  30.0 0.0 copy-done.5
  30.0 0.6 dynamic_slice.6
  30.6 1.2 %and_convert_fusion.refs_2_ = f32[1,512]{1,0:T(1,128)} fusion(s32[]{:T(128)} %bitcast.6), kind=kLoop, calls=%fused_computation.11 | loop fusion | flops 14848 | bytes 2052 | tf_op jit(solution)/shard_map/convert_element_type | solution.py:178
  31.8 1.6 %fusion.2 = bf16[16,128,512]{2,1,0:T(8,128)(2,1)} fusion(bf16[16,64,256]{2,1,0:T(8,128)(2,1)S(1)} %bitcast.18), kind=kLoop, calls=%fused_computation.4 | loop fusion | flops 8388608 | bytes 2621440 | tf_op jit(solution)/shard_map/concatenate | solution.py:167
  33.3 51.2 %all-to-all-done.refs_0_ = bf16[64,4,16,128]{3,2,1,0:T(8,128)(2,1)S(1)} async-done(((bf16[64,4,16,128]{3,2,1,0:T(8,128)(2,1)}), bf16[64,4,16,128]{3,2,1,0:T(8,128)(2,1)S(1)}, u32[]{:S(2)}, u32[]{:S(2)}) %all-to-all-start) | async-done | bytes 1048608 | tf_op jit(solution)/shard_map/all_to_all | solution.py:162
  84.6 0.0 copy-start.1
  84.6 1.0 copy-done.1
  85.6 0.0 copy-start.4
  85.6 3.8 %couple.1 = bf16[256,512]{1,0:T(8,128)(2,1)} custom-call(bf16[64,4,16,128]{3,2,1,0:T(8,128)(2,1)} %copy-done.1, bf16[8,256,512]{2,1,0:T(8,128)(2,1)} %bitcast.17, f32[1,512]{1,0:T(1,128)} %and_convert_fusion.refs_2_, bf16[512,256]{1,0:T(8,128)(2,1)} %constant.60.clone.refs_3_), custom_call_target="tpu_custom_call" | custom-call | tf_op jit(solution)/shard_map/couple/pallas_call | solution.py:181
  89.4 4.5 %all-to-all-start.1 = ((bf16[8,32,512]{2,1,0:T(8,128)(2,1)}), bf16[8,32,512]{2,1,0:T(8,128)(2,1)S(1)}, u32[]{:S(2)}, u32[]{:S(2)}) async-start(bf16[8,32,512]{2,1,0:T(8,128)(2,1)} %bitcast.19), calls=%async_computation.1 | async-start | bytes 524288 | tf_op jit(solution)/shard_map/all_to_all | solution.py:198
  93.9 0.0 copy-done
  93.9 0.1 constant_dynamic-slice_fusion
  94.0 0.1 reshape.128
  94.1 0.0 copy-done.4
  94.1 0.1 eq.18
  94.1 0.2 fusion.3
  94.4 0.1 reshape.129
  94.4 0.7 copy.16
  95.1 6.2 %all-to-all-done.1.values_ref = bf16[8,32,512]{2,1,0:T(8,128)(2,1)S(1)} async-done(((bf16[8,32,512]{2,1,0:T(8,128)(2,1)}), bf16[8,32,512]{2,1,0:T(8,128)(2,1)S(1)}, u32[]{:S(2)}, u32[]{:S(2)}) %all-to-all-start.1) | async-done | bytes 262176 | tf_op jit(solution)/shard_map/all_to_all | solution.py:198
  101.4 0.0 copy-start.2
  101.4 0.7 copy-done.2
  102.1 2.7 %convolve.1 = bf16[8,32,512]{2,1,0:T(8,128)(2,1)} custom-call(bf16[8,32,512]{2,1,0:T(8,128)(2,1)} %copy-done.2, f32[32,128]{1,0:T(8,128)} %bitcast.22), custom_call_target="tpu_custom_call" | custom-call | tf_op jit(solution)/shard_map/convolve/pallas_call | solution.py:201
  104.7 11.3 %all_to_all.15 = bf16[8,32,512]{2,1,0:T(8,128)(2,1)} all-to-all(bf16[8,32,512]{2,1,0:T(8,128)(2,1)} %convolve.1), channel_id=1, replica_groups=mesh['mom'=8,'shard'=64] {'mom'}, dimensions={0} | all-to-all | bytes 524288 | tf_op jit(solution)/shard_map/all_to_all | solution.py:208
  116.0 2.1 %back.1 = bf16[512,256]{1,0:T(8,128)(2,1)} custom-call(bf16[256,512]{1,0:T(8,128)(2,1)} %bitcast.20, bf16[512,512]{1,0:T(8,128)(2,1)} %constant.61.clone.table_ref), custom_call_target="tpu_custom_call" | custom-call | tf_op jit(solution)/shard_map/back/pallas_call | solution.py:219
  118.2 1.8 %reshape.131 = bf16[1,256,1,2,256]{4,3,1,2,0:T(2,128)(2,1)} reshape(bf16[512,256]{1,0:T(8,128)(2,1)} %back.1) | data formatting | bytes 524288 | tf_op jit(solution)/shard_map/reshape | solution.py:226
  (1 shorter events, 0.0 us)
Async XLA Ops:
  0.0 93.9 %copy-start = (f32[8,2,256]{2,1,0:T(2,128)S(1)}, f32[8,2,256]{2,1,0:T(2,128)}, u32[]{:S(2)}) copy-start(f32[8,2,256]{2,1,0:T(2,128)} %param.16) | copy-start | bytes 49156
  3.6 26.3 %copy-start.3 = (bf16[1,4,256,256]{3,2,1,0:T(8,128)(2,1)S(1)}, bf16[1,4,256,256]{3,2,1,0:T(8,128)(2,1)}, u32[]{:S(2)}) copy-start(bf16[1,4,256,256]{3,2,1,0:T(8,128)(2,1)} %param.15) | copy-start | bytes 1572868
  12.0 18.0 %copy-start.5 = (s32[64]{0:T(128)S(1)}, s32[64]{0:T(128)}, u32[]{:S(2)}) copy-start(s32[64]{0:T(128)} %orb_ref.1) | copy-start | bytes 772
  12.0 72.6 %all-to-all-start = ((bf16[64,4,16,128]{3,2,1,0:T(8,128)(2,1)}), bf16[64,4,16,128]{3,2,1,0:T(8,128)(2,1)S(1)}, u32[]{:S(2)}, u32[]{:S(2)}) async-start(bf16[64,4,16,128]{3,2,1,0:T(8,128)(2,1)} %pairs0.1), calls=%async_computation | async-start | bytes 2097152 | tf_op jit(solution)/shard_map/all_to_all | solution.py:162
  84.6 1.0 copy-start.1
  85.6 8.5 %copy-start.4 = (s32[8,8]{1,0:T(8,128)S(1)}, s32[8,8]{1,0:T(8,128)}, u32[]{:S(2)}) copy-start(s32[8,8]{1,0:T(8,128)} %param.17) | copy-start | bytes 772
  89.4 12.0 %all-to-all-start.1 = ((bf16[8,32,512]{2,1,0:T(8,128)(2,1)}), bf16[8,32,512]{2,1,0:T(8,128)(2,1)S(1)}, u32[]{:S(2)}, u32[]{:S(2)}) async-start(bf16[8,32,512]{2,1,0:T(8,128)(2,1)} %bitcast.19), calls=%async_computation.1 | async-start | bytes 524288 | tf_op jit(solution)/shard_map/all_to_all | solution.py:198
  101.4 0.7 copy-start.2

commit v2 on v1

v2 whole, which is shorter than its diff:
```python
import jax
import jax.numpy as jnp
import numpy as np
from jax import lax
from jax.experimental import pallas as pl
from jax.experimental.pallas import tpu as pltpu
from jax.sharding import PartitionSpec as P

NORB = 16
ATL = 8
NBR = 4
ENERGIES = 256
LAYERS = 8
ORB = 128
PAIR = 256
ATOMS = 64
KPTS = 8
STEP_LAYERS = 2

F32 = jnp.float32
BF16 = jnp.bfloat16
VMEM_SPEC = pl.BlockSpec(memory_space=pltpu.VMEM)


def dft_tables(length):
    counter = np.arange(length)
    angles = (counter[:, None] * counter[None, :] % length) * (2.0 * np.pi / length)
    return np.cos(angles).astype(jnp.bfloat16), np.sin(angles).astype(jnp.bfloat16)


def pairs_kernel(occ_ref, nbr_ref, orb_ref, green_ref, broad_ref, out_ref, mix_ref):
    step = pl.program_id(0)
    energies = green_ref.shape[1]
    layers = green_ref.shape[2]

    @pl.when(step == 0)
    def _():
        mix_ref[:ORB, :ORB] = broad_ref[0]
        mix_ref[:ORB, ORB:] = broad_ref[1]
        mix_ref[ORB:, :ORB] = -broad_ref[1]
        mix_ref[ORB:, ORB:] = broad_ref[0]

    lane = lax.broadcasted_iota(jnp.int32, (1, ORB), 1)
    slot = (lane // NORB) % NBR
    column = lane % NORB
    source = lax.broadcasted_iota(jnp.int32, (ORB, ORB), 0)
    row = lax.broadcasted_iota(jnp.int32, (energies * NORB, ORB), 0) % NORB
    low = lax.broadcasted_iota(jnp.int32, (energies * NORB, ORB), 1) < ORB // 2
    for l in range(layers):
        rows = []
        for e in range(energies):
            rows.append(jnp.concatenate([green_ref[0, e, l, 0], green_ref[0, e, l, 1]], axis=1))
        left = jnp.dot(jnp.concatenate(rows, axis=0), mix_ref[...], preferred_element_type=F32)
        left = left.astype(BF16)
        full = []
        for e in range(energies):
            green_re = green_ref[0, e, l, 0]
            green_im = green_ref[0, e, l, 1]
            partner = jnp.concatenate(
                [
                    jnp.concatenate([green_re, green_im], axis=1),
                    jnp.concatenate([-green_im, green_re], axis=1),
                ],
                axis=0,
            )
            block = lax.dot_general(
                left[e * ORB : (e + 1) * ORB],
                partner,
                (((1,), (1,)), ((), ())),
                preferred_element_type=F32,
            )
            full.append((block * occ_ref[0, e]).astype(BF16))
        for a in range(ATL):
            atom = (step * layers + l) * ATL + a
            target = jnp.full((1, ORB), -1, jnp.int32)
            for n in range(NBR):
                partner_atom = nbr_ref[n, atom]
                start = (partner_atom % ATL) * NORB
                chosen = (slot == n) & (column < orb_ref[partner_atom])
                target = jnp.where(chosen, start + column, target)
            select = jnp.where(source == target, 1.0, 0.0).astype(BF16)
            part_rows = [
                full[e][a * NORB : (a + 1) * NORB, p * ORB : (p + 1) * ORB]
                for p in range(2)
                for e in range(energies)
            ]
            picked = jnp.dot(
                jnp.concatenate(part_rows, axis=0), select, preferred_element_type=F32
            )
            half = energies * NORB
            merged = jnp.where(low, picked[:half], picked[half:])
            merged = jnp.where(row < orb_ref[atom], merged, 0.0).astype(BF16)
            out_ref[l * ATL + a] = merged.reshape(energies, NORB, ORB)


def make_pairs(green_ret, broadening, occupation, neighbours, orbitals):
    energies = green_ret.shape[1]
    smem = pl.BlockSpec(memory_space=pltpu.SMEM)
    return pl.pallas_call(
        pairs_kernel,
        grid=(LAYERS // STEP_LAYERS,),
        in_specs=[
            smem,
            smem,
            smem,
            pl.BlockSpec((1, energies, STEP_LAYERS, 2, ORB, ORB), lambda s: (0, 0, s, 0, 0, 0)),
            pl.BlockSpec((2, ORB, ORB), lambda s: (0, 0, 0)),
        ],
        out_specs=pl.BlockSpec((STEP_LAYERS * ATL, energies, NORB, ORB), lambda s: (s, 0, 0, 0)),
        out_shape=jax.ShapeDtypeStruct((ATOMS, energies, NORB, ORB), BF16),
        scratch_shapes=[pltpu.VMEM((2 * ORB, 2 * ORB), BF16)],
        name="pairs",
    )(occupation, neighbours.T, orbitals, green_ret, broadening)


def couple_kernel(arrived_ref, weight_ref, mask_ref, table_ref, out_ref, wide):
    wide[...] = arrived_ref[...].reshape(ENERGIES * NORB, ORB).astype(F32)
    rows = [wide[pl.ds(i, ENERGIES, stride=NORB), :].astype(BF16) for i in range(NORB)]
    total = jnp.dot(
        jnp.concatenate(rows, axis=1), weight_ref[...], preferred_element_type=F32
    )
    coupled = (total * mask_ref[...]).astype(BF16)
    spectra = jnp.dot(table_ref[...], coupled, preferred_element_type=F32)
    out_ref[:, :PAIR] = (spectra[:ENERGIES, :PAIR] + spectra[ENERGIES:, PAIR:]).astype(BF16)
    out_ref[:, PAIR:] = (spectra[:ENERGIES, PAIR:] - spectra[ENERGIES:, :PAIR]).astype(BF16)


def convolve_kernel(values_ref, high_ref, low_ref, out_ref):
    for block in range(high_ref.shape[0]):
        times = slice(block * NORB, (block + 1) * NORB)
        values = jnp.concatenate(
            [
                values_ref[k, times, p * PAIR : (p + 1) * PAIR]
                for p in range(2)
                for k in range(KPTS)
            ],
            axis=0,
        )
        sums = jnp.dot(high_ref[block], values, preferred_element_type=F32) + jnp.dot(
            low_ref[block], values, preferred_element_type=F32
        )
        for k in range(KPTS):
            for p in range(2):
                first = (k * 2 + p) * NORB
                out_ref[k, times, p * PAIR : (p + 1) * PAIR] = sums[first : first + NORB].astype(
                    BF16
                )


def back_kernel(values_ref, table_ref, out_ref):
    values = jnp.concatenate([values_ref[:, :PAIR], values_ref[:, PAIR:]], axis=0)
    result = jnp.dot(table_ref[...], values, preferred_element_type=F32)
    result = (result * (1.0 / ENERGIES)).astype(BF16)
    out_ref[0, :, 0] = result.reshape(ENERGIES, 2, PAIR)


def in_vmem(value):
    return pltpu.with_memory_space_constraint(value, pltpu.VMEM)


def local(
    green_ret, broadening, occupation, neighbours, orbitals, coupling, phonon, mode_table
):
    highest = lax.Precision.HIGHEST
    pairs = make_pairs(green_ret, broadening, occupation, neighbours, orbitals)
    arrived = lax.all_to_all(pairs, "shard", split_axis=0, concat_axis=0, tiled=True)

    parts = coupling.reshape(NBR, NORB, NORB, PAIR).transpose(1, 0, 2, 3)
    parts = parts.reshape(NORB, NBR * NORB, PAIR)
    zeros = jnp.zeros_like(parts)
    weights = jnp.concatenate(
        [
            jnp.concatenate([parts, zeros], axis=2),
            jnp.concatenate([zeros, parts], axis=2),
        ],
        axis=1,
    ).reshape(2 * NBR * PAIR, 2 * PAIR)
    own_atom = lax.axis_index("shard")
    own_count = lax.dynamic_slice_in_dim(orbitals, own_atom, 1)[0]
    pair_index = jnp.arange(2 * PAIR, dtype=jnp.int32) % PAIR
    own_mask = (pair_index // NORB < own_count) & (pair_index % NORB < own_count)
    own_mask = own_mask.astype(F32)[None, :]
    cos_table, sin_table = dft_tables(ENERGIES)
    forward = jnp.asarray(np.concatenate([cos_table, sin_table], axis=0))
    timed = pl.pallas_call(
        couple_kernel,
        in_specs=[VMEM_SPEC] * 4,
        out_specs=VMEM_SPEC,
        out_shape=pltpu.VMEM((ENERGIES, 2 * PAIR), BF16),
        scratch_shapes=[pltpu.VMEM((ENERGIES * NORB, ORB), F32)],
        compiler_params=pltpu.CompilerParams(vmem_limit_bytes=24 * 2**20),
        name="couple",
    )(in_vmem(arrived), in_vmem(weights), in_vmem(own_mask), in_vmem(forward))

    span = ENERGIES // KPTS
    own_momentum = lax.axis_index("mom")
    own_phonon = lax.dynamic_slice_in_dim(phonon, own_momentum * span, span, 2)
    mode_ids = jnp.arange(phonon.shape[0], dtype=jnp.int32)
    one_hot = (mode_table.reshape(-1, 1) == mode_ids[None, :]).astype(F32)
    kernel = jnp.dot(one_hot, own_phonon.reshape(phonon.shape[0], -1), precision=highest)
    kernel = kernel.reshape(KPTS, KPTS, 2, span // NORB, NORB)
    kernel_re = kernel[:, :, 0].transpose(2, 0, 3, 1)
    kernel_im = kernel[:, :, 1].transpose(2, 0, 3, 1)
    terms = jnp.stack(
        [
            jnp.stack([kernel_re, -kernel_im], axis=3),
            jnp.stack([kernel_im, kernel_re], axis=3),
        ],
        axis=2,
    )
    same = jnp.eye(NORB, dtype=F32)[:, None, None, :]
    kernels = (terms[..., None] * same).reshape(span // NORB, 2 * KPTS * NORB, 2 * KPTS * NORB)
    high = kernels.astype(BF16)
    low = (kernels - high.astype(F32)).astype(BF16)

    moved = lax.all_to_all(
        timed.reshape(KPTS, span, 2 * PAIR), "mom", split_axis=0, concat_axis=0, tiled=True
    )
    convolved = pl.pallas_call(
        convolve_kernel,
        in_specs=[VMEM_SPEC] * 3,
        out_specs=VMEM_SPEC,
        out_shape=pltpu.VMEM((KPTS, span, 2 * PAIR), BF16),
        compiler_params=pltpu.CompilerParams(vmem_limit_bytes=12 * 2**20),
        name="convolve",
    )(in_vmem(moved), in_vmem(high), in_vmem(low))
    returned = lax.all_to_all(convolved, "mom", split_axis=0, concat_axis=0, tiled=True)

    wide_cos = cos_table.astype(np.float32)
    wide_sin = sin_table.astype(np.float32)
    backward = np.stack(
        [
            np.concatenate([wide_cos, -wide_sin], axis=1),
            np.concatenate([wide_sin, wide_cos], axis=1),
        ],
        axis=1,
    ).reshape(2 * ENERGIES, 2 * ENERGIES)
    return pl.pallas_call(
        back_kernel,
        in_specs=[VMEM_SPEC] * 2,
        out_specs=VMEM_SPEC,
        out_shape=jax.ShapeDtypeStruct((1, ENERGIES, 1, 2, PAIR), BF16),
        compiler_params=pltpu.CompilerParams(vmem_limit_bytes=12 * 2**20),
        name="back",
    )(in_vmem(returned.reshape(ENERGIES, 2 * PAIR)), in_vmem(jnp.asarray(backward, dtype=BF16)))


def solution(mesh):
    in_specs = (
        P("mom", "shard", None, None, None, None),
        P(),
        P("mom", "shard"),
        P(),
        P(),
        P("shard", None, None, None),
        P(),
        P(),
    )
    out_specs = P("mom", None, "shard", None, None)
    return jax.shard_map(local, mesh=mesh, in_specs=in_specs, out_specs=out_specs, check_vma=False)
```

time: 121 us -> 105 us (0.87)
  waiting for transfers between devices: 57.5 us -> 48.9 us
  Pallas kernels: 17 us -> 9.79 us
  local copies, waits for them, and re-layouts: 7.26 us -> 10.7 us
  other arithmetic: 4.22 us -> 2.11 us
  blocking collectives: 11.3 us -> 9.82 us
    all_to_all x1, waiting for transfers between devices: 51.2 us -> 42.7 us  [local(): lax.all_to_all(pairs, 'shard', split_axis=0, concat_axis=0, tiled=True)]
    mul x0 -> x4, local copies, waits for them, and re-layouts: none -> 8.52 us  [local(): terms[..., None] * same]
    pallas_call x3, Pallas kernels: 14.9 us -> 8.78 us  [the longest x1 6.52 us: make_pairs(): pl.pallas_call(pairs_kernel, grid=(LAYERS // STEP_LAYERS,), in_specs=[sme...]
    unnamed x13 -> x10, local copies, waits for them, and re-layouts: 3.09 us -> 0.02 us
    reshape x3 -> x0, local copies, waits for them, and re-layouts: 2.5 us -> none  [the longest x1 1.75 us: local(): return result.reshape(1, ENERGIES, 1, 2, PAIR)]
    all_to_all x1, blocking collectives: 11.3 us -> 9.82 us  [local(): lax.all_to_all(convolved, 'mom', split_axis=0, concat_axis=0, tiled=True)]
    concatenate x1, other arithmetic: 1.56 us -> 0.21 us  [local(): jnp.concatenate([jnp.concatenate([parts, zeros], axis=2), jnp.concatenate...]
  transfers between devices with their start and end apart: 2 -> 2, of which waited for: 2 -> 2; matrix products, arithmetic and copies ran while one was open for 4% -> 13% of each run, Pallas kernels for 0% -> 0%
where the time goes in v2:
time: 105 us; the launch traced here: 104 us
  waiting for transfers between devices  48.9 us (47%)
  starting transfers between devices  22.4 us (21%)
  local copies, waits for them, and re-layouts  10.7 us (10%)
  blocking collectives  9.82 us (9%)
  Pallas kernels  9.79 us (9%)
  other arithmetic  2.11 us (2%)
    all_to_all x1, waiting for transfers between devices, local(): lax.all_to_all(pairs, 'shard', split_axis=0, concat_axis=0, tiled=True)  42.7 us
    all_to_all x1, starting transfers between devices, local(): lax.all_to_all(pairs, 'shard', split_axis=0, concat_axis=0, tiled=True)  17.8 us
    all_to_all x1, blocking collectives, local(): lax.all_to_all(convolved, 'mom', split_axis=0, concat_axis=0, tiled=True)  9.82 us
    mul x4, local copies, waits for them, and re-layouts, local(): terms[..., None] * same  8.52 us
    pallas_call x1, Pallas kernels, make_pairs(): pl.pallas_call(pairs_kernel, grid=(LAYERS // STEP_LAYERS,), in_specs=[sme...  6.52 us
    all_to_all x1, waiting for transfers between devices, local(): lax.all_to_all(timed.reshape(KPTS, span, 2 * PAIR), 'mom', split_axis=0,...  6.27 us
    all_to_all x1, starting transfers between devices, local(): lax.all_to_all(timed.reshape(KPTS, span, 2 * PAIR), 'mom', split_axis=0,...  4.64 us
  transfers between devices with their start and end apart: 2, of which 2 were waited for; matrix products, arithmetic and copies ran while one was open for 13% of the time, Pallas kernels for 0%

profile of v2, /device:TPU:64, one launch (start us, length us, event | category | flops | bytes accessed | tf_op | source)
XLA Modules:
  0.0 104.2 jit_solution(15255878958709165472)
XLA Ops:
  0.0 0.0 copy-start
  0.0 0.0 copy-start.3
  0.0 6.5 %pairs.1 = bf16[64,4,16,128]{3,2,1,0:T(8,128)(2,1)} custom-call(f32[1,4]{1,0:T(1,128)} %occ_ref.1, s32[4,64]{1,0:T(4,128)} %bitcast.54, s32[64]{0:T(128)} %orb_ref.1, bf16[1,4,8,2,128,128]{5,4,3,2,1,0:T(8,128)(2,1)} %green_ref.1, bf16[2,128,128]{2,1,0:T(8,128)(2,1)} %broad_ref.1), custom_call_target="tpu_custom_call" | custom-call | tf_op jit(solution)/shard_map/pairs/pallas_call | solution.py:99
  6.5 17.8 %all-to-all-start = ((bf16[64,4,16,128]{3,2,1,0:T(8,128)(2,1)}), bf16[64,4,16,128]{3,2,1,0:T(8,128)(2,1)S(1)}, u32[]{:S(2)}, u32[]{:S(2)}) async-start(bf16[64,4,16,128]{3,2,1,0:T(8,128)(2,1)} %pairs.1), calls=%async_computation | async-start | bytes 2097152 | tf_op jit(solution)/shard_map/all_to_all | solution.py:166
  24.3 0.0 copy-done
  24.3 0.1 constant_dynamic-slice_fusion
  24.4 0.1 reshape.157
  24.5 0.1 dot_general.8
  24.6 0.0 copy-done.3
  24.6 0.2 fusion.5
  24.9 0.3 copy.17
  25.2 2.6 %mul.24 = f32[2,8,2,16,2,8,16]{6,5,4,3,2,1,0:T(8,128)} broadcast(f32[2,8,2,16,2,8]{5,4,3,2,1,0:T(2,128)S(1)} %copy.17), dimensions={0,1,2,3,4,5} | broadcast | bytes 557056 | tf_op jit(solution)/shard_map/mul | solution.py:212
  27.8 4.2 %mul.25 = f32[2,256,256]{2,1,0:T(8,128)} reshape(f32[2,8,2,16,2,8,16]{6,5,4,3,2,1,0:T(8,128)} %mul.24) | data formatting | bytes 1048576 | tf_op jit(solution)/shard_map/mul | solution.py:212
  32.0 0.0 copy-start.4
  32.0 0.2 mul.26
  32.2 1.5 %mul.27 = f32[256,256]{1,0:T(8,128)} reshape(f32[8,2,16,2,8,16]{5,4,3,2,1,0:T(8,128)S(1)} %mul.26) | data formatting | bytes 524288 | tf_op jit(solution)/shard_map/mul | solution.py:212
  33.8 0.0 copy-start.2
  33.8 0.0 copy-done.4
  33.8 0.6 dynamic_slice.6
  34.3 1.1 %copy.14 = bf16[16,4,16,256]{3,2,1,0:T(8,128)(2,1)S(1)} copy(bf16[16,4,16,256]{3,2,0,1:T(8,128)(2,1)} %bitcast.52) | data formatting | bytes 1048576 | tf_op jit(solution)/shard_map/transpose | solution.py:168
  35.4 0.7 and_convert_fusion.mask_ref
  36.1 0.2 fusion.2
  36.3 42.7 %all-to-all-done.arrived_ref = bf16[64,4,16,128]{3,2,1,0:T(8,128)(2,1)S(1)} async-done(((bf16[64,4,16,128]{3,2,1,0:T(8,128)(2,1)}), bf16[64,4,16,128]{3,2,1,0:T(8,128)(2,1)S(1)}, u32[]{:S(2)}, u32[]{:S(2)}) %all-to-all-start) | async-done | bytes 1048608 | tf_op jit(solution)/shard_map/all_to_all | solution.py:166
  79.0 0.0 copy-done.2
  79.0 2.0 %couple.1 = bf16[256,512]{1,0:T(8,128)(2,1)} custom-call(bf16[64,4,16,128]{3,2,1,0:T(8,128)(2,1)S(1)} %all-to-all-done.arrived_ref, bf16[2048,512]{1,0:T(8,128)(2,1)S(1)} %bitcast.49, f32[1,512]{1,0:T(1,128)S(1)} %and_convert_fusion.mask_ref, bf16[512,256]{1,0:T(8,128)(2,1)S(1)} %copy-done.2), custom_call_target="tpu_custom_call" | custom-call | tf_op jit(solution)/shard_map/couple/pallas_call | solution.py:185
  80.9 0.0 copy-start.1
  80.9 4.6 %all-to-all-start.1 = ((bf16[8,32,512]{2,1,0:T(8,128)(2,1)}), bf16[8,32,512]{2,1,0:T(8,128)(2,1)S(1)}, u32[]{:S(2)}, u32[]{:S(2)}) async-start(bf16[8,32,512]{2,1,0:T(8,128)(2,1)} %bitcast.6), calls=%async_computation.1 | async-start | bytes 524288 | tf_op jit(solution)/shard_map/all_to_all | solution.py:216
  85.6 1.2 %subtract_convert_fusion = (bf16[2,256,256]{2,1,0:T(8,128)(2,1)S(1)}, bf16[2,256,256]{2,1,0:T(8,128)(2,1)S(1)}) fusion(f32[2,256,256]{2,1,0:T(8,128)} %mul.25, f32[256,256]{1,0:T(8,128)} %mul.27), kind=kLoop, calls=%fused_computation.5 | loop fusion | flops 655360 | bytes 1310720 | tf_op jit(solution)/shard_map/convert_element_type | solution.py:214
  86.8 6.3 %all-to-all-done.1.values_ref = bf16[8,32,512]{2,1,0:T(8,128)(2,1)S(1)} async-done(((bf16[8,32,512]{2,1,0:T(8,128)(2,1)}), bf16[8,32,512]{2,1,0:T(8,128)(2,1)S(1)}, u32[]{:S(2)}, u32[]{:S(2)}) %all-to-all-start.1) | async-done | bytes 262176 | tf_op jit(solution)/shard_map/all_to_all | solution.py:216
  93.0 0.3 convolve.1
  93.4 9.8 %all_to_all.15 = bf16[8,32,512]{2,1,0:T(8,128)(2,1)S(1)} all-to-all(bf16[8,32,512]{2,1,0:T(8,128)(2,1)S(1)} %convolve.1), channel_id=1, replica_groups=mesh['mom'=8,'shard'=64] {'mom'}, dimensions={0} | all-to-all | bytes 524288 | tf_op jit(solution)/shard_map/all_to_all | solution.py:227
  103.2 0.0 copy-done.1
  103.2 1.0 back.1
  (5 shorter events, 0.1 us)
Async XLA Ops:
  0.0 24.3 %copy-start = (f32[8,2,256]{2,1,0:T(2,128)S(1)}, f32[8,2,256]{2,1,0:T(2,128)}, u32[]{:S(2)}) copy-start(f32[8,2,256]{2,1,0:T(2,128)} %param.16) | copy-start | bytes 49156
  0.0 24.6 %copy-start.3 = (s32[8,8]{1,0:T(8,128)S(1)}, s32[8,8]{1,0:T(8,128)}, u32[]{:S(2)}) copy-start(s32[8,8]{1,0:T(8,128)} %param.17) | copy-start | bytes 772
  6.5 72.5 %all-to-all-start = ((bf16[64,4,16,128]{3,2,1,0:T(8,128)(2,1)}), bf16[64,4,16,128]{3,2,1,0:T(8,128)(2,1)S(1)}, u32[]{:S(2)}, u32[]{:S(2)}) async-start(bf16[64,4,16,128]{3,2,1,0:T(8,128)(2,1)} %pairs.1), calls=%async_computation | async-start | bytes 2097152 | tf_op jit(solution)/shard_map/all_to_all | solution.py:166
  32.0 1.8 %copy-start.4 = (s32[64]{0:T(128)S(1)}, s32[64]{0:T(128)}, u32[]{:S(2)}) copy-start(s32[64]{0:T(128)} %orb_ref.1) | copy-start | bytes 772
  33.8 45.2 %copy-start.2 = (bf16[512,256]{1,0:T(8,128)(2,1)S(1)}, bf16[512,256]{1,0:T(8,128)(2,1)}, u32[]{:S(2)}) copy-start(bf16[512,256]{1,0:T(8,128)(2,1)} %constant.60.clone.table_ref) | copy-start | bytes 786436
  80.9 22.2 %copy-start.1 = (bf16[512,512]{1,0:T(8,128)(2,1)S(1)}, bf16[512,512]{1,0:T(8,128)(2,1)}, u32[]{:S(2)}) copy-start(bf16[512,512]{1,0:T(8,128)(2,1)} %constant.61.clone.table_ref) | copy-start | bytes 1572868
  80.9 12.1 %all-to-all-start.1 = ((bf16[8,32,512]{2,1,0:T(8,128)(2,1)}), bf16[8,32,512]{2,1,0:T(8,128)(2,1)S(1)}, u32[]{:S(2)}, u32[]{:S(2)}) async-start(bf16[8,32,512]{2,1,0:T(8,128)(2,1)} %bitcast.6), calls=%async_computation.1 | async-start | bytes 524288 | tf_op jit(solution)/shard_map/all_to_all | solution.py:216

commit v3 on v2

v3 whole, which is shorter than its diff:
```python
import jax
import jax.numpy as jnp
import numpy as np
from jax import lax
from jax.experimental import pallas as pl
from jax.experimental.pallas import tpu as pltpu
from jax.sharding import PartitionSpec as P

NORB = 16
ATL = 8
NBR = 4
ENERGIES = 256
LAYERS = 8
ORB = 128
PAIR = 256
ATOMS = 64
KPTS = 8
STEP_LAYERS = 4

F32 = jnp.float32
BF16 = jnp.bfloat16
VMEM_SPEC = pl.BlockSpec(memory_space=pltpu.VMEM)


def dft_tables(length):
    counter = np.arange(length)
    angles = (counter[:, None] * counter[None, :] % length) * (2.0 * np.pi / length)
    return np.cos(angles).astype(jnp.bfloat16), np.sin(angles).astype(jnp.bfloat16)


def pairs_kernel(occ_ref, nbr_ref, green_ref, broad_ref, out_ref, mix_ref, left_ref, full_ref):
    step = pl.program_id(0)
    energies = green_ref.shape[1]
    layers = green_ref.shape[2]

    @pl.when(step == 0)
    def _():
        mix_ref[:ORB, :ORB] = broad_ref[0]
        mix_ref[:ORB, ORB:] = broad_ref[1]
        mix_ref[ORB:, :ORB] = -broad_ref[1]
        mix_ref[ORB:, ORB:] = broad_ref[0]

    rows = [
        jnp.concatenate([green_ref[0, e, l, 0], green_ref[0, e, l, 1]], axis=1)
        for l in range(layers)
        for e in range(energies)
    ]
    left = jnp.dot(jnp.concatenate(rows, axis=0), mix_ref[...], preferred_element_type=F32)
    left_ref[...] = left.astype(BF16)
    for l in range(layers):
        for e in range(energies):
            block = slice((l * energies + e) * ORB, (l * energies + e + 1) * ORB)
            green_re = green_ref[0, e, l, 0]
            green_im = green_ref[0, e, l, 1]
            partner = jnp.concatenate(
                [
                    jnp.concatenate([green_re, green_im], axis=1),
                    jnp.concatenate([-green_im, green_re], axis=1),
                ],
                axis=0,
            )
            product = lax.dot_general(
                left_ref[block], partner, (((1,), (1,)), ((), ())), preferred_element_type=F32
            )
            full_ref[block] = (product * occ_ref[0, e]).astype(BF16)

    lane = lax.broadcasted_iota(jnp.int32, (1, ORB), 1)
    slot = (lane // NORB) % NBR
    column = lane % NORB
    source = lax.broadcasted_iota(jnp.int32, (ORB, ORB), 0).astype(F32).astype(BF16)
    half = energies * NORB
    low = lax.broadcasted_iota(jnp.int32, (half, ORB), 1) < ORB // 2
    one = jnp.ones((ORB, ORB), BF16)
    zero = jnp.zeros((ORB, ORB), BF16)
    for l in range(layers):
        for a in range(ATL):
            atom = (step * layers + l) * ATL + a
            starts = [(nbr_ref[n, atom] & (ATL - 1)) * NORB for n in range(NBR)]
            target = jnp.where(
                slot < 2,
                jnp.where(slot == 0, starts[0], starts[1]),
                jnp.where(slot == 2, starts[2], starts[3]),
            )
            target = (target + column).astype(F32).astype(BF16)
            select = jnp.where(source == target, one, zero)
            part_rows = [
                full_ref[
                    (l * energies + e) * ORB + a * NORB : (l * energies + e) * ORB + (a + 1) * NORB,
                    p * ORB : (p + 1) * ORB,
                ]
                for p in range(2)
                for e in range(energies)
            ]
            picked = jnp.dot(
                jnp.concatenate(part_rows, axis=0), select, preferred_element_type=F32
            )
            merged = jnp.where(low, picked[:half], picked[half:]).astype(BF16)
            out_ref[l * ATL + a] = merged.reshape(energies, NORB, ORB)


def make_pairs(green_ret, broadening, occupation, neighbours):
    energies = green_ret.shape[1]
    smem = pl.BlockSpec(memory_space=pltpu.SMEM)
    rows = STEP_LAYERS * energies * ORB
    return pl.pallas_call(
        pairs_kernel,
        grid=(LAYERS // STEP_LAYERS,),
        in_specs=[
            smem,
            smem,
            pl.BlockSpec((1, energies, STEP_LAYERS, 2, ORB, ORB), lambda s: (0, 0, s, 0, 0, 0)),
            pl.BlockSpec((2, ORB, ORB), lambda s: (0, 0, 0)),
        ],
        out_specs=pl.BlockSpec((STEP_LAYERS * ATL, energies, NORB, ORB), lambda s: (s, 0, 0, 0)),
        out_shape=jax.ShapeDtypeStruct((ATOMS, energies, NORB, ORB), BF16),
        scratch_shapes=[
            pltpu.VMEM((2 * ORB, 2 * ORB), BF16),
            pltpu.VMEM((rows, 2 * ORB), BF16),
            pltpu.VMEM((rows, 2 * ORB), BF16),
        ],
        name="pairs",
    )(occupation, neighbours.T, green_ret, broadening)


def couple_kernel(arrived_ref, weight_ref, table_hbm, out_ref, wide, table_ref, table_sem):
    table_copy = pltpu.make_async_copy(table_hbm, table_ref, table_sem)
    table_copy.start()
    wide[...] = arrived_ref[...].reshape(ENERGIES * NORB, ORB).astype(F32)
    rows = [wide[pl.ds(i, ENERGIES, stride=NORB), :].astype(BF16) for i in range(NORB)]
    total = jnp.dot(
        jnp.concatenate(rows, axis=1), weight_ref[...], preferred_element_type=F32
    )
    coupled = total.astype(BF16)
    table_copy.wait()
    spectra = jnp.dot(table_ref[...], coupled, preferred_element_type=F32)
    out_ref[:, :PAIR] = (spectra[:ENERGIES, :PAIR] + spectra[ENERGIES:, PAIR:]).astype(BF16)
    out_ref[:, PAIR:] = (spectra[:ENERGIES, PAIR:] - spectra[ENERGIES:, :PAIR]).astype(BF16)


def convolve_kernel(values_ref, high_ref, low_ref, out_ref):
    for block in range(high_ref.shape[0]):
        times = slice(block * NORB, (block + 1) * NORB)
        values = jnp.concatenate(
            [
                values_ref[k, times, p * PAIR : (p + 1) * PAIR]
                for p in range(2)
                for k in range(KPTS)
            ],
            axis=0,
        )
        sums = jnp.dot(high_ref[block], values, preferred_element_type=F32) + jnp.dot(
            low_ref[block], values, preferred_element_type=F32
        )
        for k in range(KPTS):
            for p in range(2):
                first = (k * 2 + p) * NORB
                out_ref[k, times, p * PAIR : (p + 1) * PAIR] = sums[first : first + NORB].astype(
                    BF16
                )


def back_kernel(values_ref, table_ref, out_ref):
    values = jnp.concatenate([values_ref[:, :PAIR], values_ref[:, PAIR:]], axis=0)
    result = jnp.dot(table_ref[...], values, preferred_element_type=F32)
    result = (result * (1.0 / ENERGIES)).astype(BF16)
    out_ref[0, :, 0] = result.reshape(ENERGIES, 2, PAIR)


def in_vmem(value):
    return pltpu.with_memory_space_constraint(value, pltpu.VMEM)


def in_hbm(value):
    return pltpu.with_memory_space_constraint(value, pltpu.HBM)


def local(
    green_ret, broadening, occupation, neighbours, orbitals, coupling, phonon, mode_table
):
    highest = lax.Precision.HIGHEST
    pairs = make_pairs(green_ret, broadening, occupation, neighbours)
    arrived = lax.all_to_all(pairs, "shard", split_axis=0, concat_axis=0, tiled=True)

    own_atom = lax.axis_index("shard")
    own_count = lax.dynamic_slice_in_dim(orbitals, own_atom, 1)[0]
    own_slots = lax.dynamic_slice_in_dim(neighbours, own_atom, 1)[0]
    slot_atoms = own_slots[:, None] == jnp.arange(ATOMS, dtype=jnp.int32)[None, :]
    slot_counts = jnp.sum(jnp.where(slot_atoms, orbitals[None, :], 0), axis=1)
    counter = jnp.arange(NORB, dtype=jnp.int32)
    pair_index = jnp.arange(PAIR, dtype=jnp.int32)
    own_mask = (pair_index // NORB < own_count) & (pair_index % NORB < own_count)
    keep = (
        (counter < own_count)[:, None, None, None]
        & (counter[None, :] < slot_counts[:, None])[None, :, :, None]
        & own_mask[None, None, None, :]
    )
    parts = coupling.reshape(NBR, NORB, NORB, PAIR).transpose(1, 0, 2, 3)
    parts = jnp.where(keep, parts, jnp.zeros_like(parts)).reshape(NORB, NBR * NORB, PAIR)
    zeros = jnp.zeros_like(parts)
    weights = jnp.concatenate(
        [
            jnp.concatenate([parts, zeros], axis=2),
            jnp.concatenate([zeros, parts], axis=2),
        ],
        axis=1,
    ).reshape(2 * NBR * PAIR, 2 * PAIR)
    span = ENERGIES // KPTS
    own_momentum = lax.axis_index("mom")
    own_phonon = lax.dynamic_slice_in_dim(phonon, own_momentum * span, span, 2)
    mode_ids = jnp.arange(phonon.shape[0], dtype=jnp.int32)
    one_hot = (mode_table.reshape(-1, 1) == mode_ids[None, :]).astype(F32)
    kernel = jnp.dot(one_hot, own_phonon.reshape(phonon.shape[0], -1), precision=highest)
    kernel = kernel.reshape(KPTS, KPTS, 2, span // NORB, NORB)
    kernel_re = kernel[:, :, 0].transpose(2, 0, 3, 1)
    kernel_im = kernel[:, :, 1].transpose(2, 0, 3, 1)
    terms = jnp.stack(
        [
            jnp.stack([kernel_re, -kernel_im], axis=3),
            jnp.stack([kernel_im, kernel_re], axis=3),
        ],
        axis=2,
    )
    same = jnp.eye(NORB, dtype=F32)[:, None, None, :]
    kernels = (terms[..., None] * same).reshape(span // NORB, 2 * KPTS * NORB, 2 * KPTS * NORB)
    high = kernels.astype(BF16)
    low = (kernels - high.astype(F32)).astype(BF16)
    cos_table, sin_table = dft_tables(ENERGIES)
    forward = np.concatenate([cos_table, sin_table], axis=0)
    wide_cos = cos_table.astype(np.float32)
    wide_sin = sin_table.astype(np.float32)
    backward = np.stack(
        [
            np.concatenate([wide_cos, -wide_sin], axis=1),
            np.concatenate([wide_sin, wide_cos], axis=1),
        ],
        axis=1,
    ).reshape(2 * ENERGIES, 2 * ENERGIES)
    arrived, weights, high, low = lax.optimization_barrier((arrived, weights, high, low))
    timed = pl.pallas_call(
        couple_kernel,
        in_specs=[VMEM_SPEC, VMEM_SPEC, pl.BlockSpec(memory_space=pltpu.HBM)],
        out_specs=VMEM_SPEC,
        out_shape=pltpu.VMEM((ENERGIES, 2 * PAIR), BF16),
        scratch_shapes=[
            pltpu.VMEM((ENERGIES * NORB, ORB), F32),
            pltpu.VMEM((2 * ENERGIES, ENERGIES), BF16),
            pltpu.SemaphoreType.DMA,
        ],
        compiler_params=pltpu.CompilerParams(vmem_limit_bytes=24 * 2**20),
        name="couple",
    )(in_vmem(arrived), in_vmem(weights), in_hbm(jnp.asarray(forward)))

    moved = lax.all_to_all(
        timed.reshape(KPTS, span, 2 * PAIR), "mom", split_axis=0, concat_axis=0, tiled=True
    )
    convolved = pl.pallas_call(
        convolve_kernel,
        in_specs=[VMEM_SPEC] * 3,
        out_specs=VMEM_SPEC,
        out_shape=pltpu.VMEM((KPTS, span, 2 * PAIR), BF16),
        compiler_params=pltpu.CompilerParams(vmem_limit_bytes=12 * 2**20),
        name="convolve",
    )(in_vmem(moved), in_vmem(high), in_vmem(low))
    returned = lax.all_to_all(convolved, "mom", split_axis=0, concat_axis=0, tiled=True)

    return pl.pallas_call(
        back_kernel,
        in_specs=[VMEM_SPEC] * 2,
        out_specs=VMEM_SPEC,
        out_shape=jax.ShapeDtypeStruct((1, ENERGIES, 1, 2, PAIR), BF16),
        compiler_params=pltpu.CompilerParams(vmem_limit_bytes=12 * 2**20),
        name="back",
    )(in_vmem(returned.reshape(ENERGIES, 2 * PAIR)), in_vmem(jnp.asarray(backward, dtype=BF16)))


def solution(mesh):
    in_specs = (
        P("mom", "shard", None, None, None, None),
        P(),
        P("mom", "shard"),
        P(),
        P(),
        P("shard", None, None, None),
        P(),
        P(),
    )
    out_specs = P("mom", None, "shard", None, None)
    return jax.shard_map(local, mesh=mesh, in_specs=in_specs, out_specs=out_specs, check_vma=False)
```

time: 105 us -> 103 us (0.981)
  blocking collectives: 9.82 us -> 21.6 us
  waiting for transfers between devices: 48.9 us -> 39.8 us
  starting transfers between devices: 22.4 us -> 17.8 us
  other arithmetic: 2.11 us -> 3.81 us
  Pallas kernels: 9.79 us -> 8.19 us
    all_to_all x0 -> x1, blocking collectives: none -> 11.8 us  [local(): lax.all_to_all(timed.reshape(KPTS, span, 2 * PAIR), 'mom', split_axis=0,...]
    all_to_all x1 -> x0, waiting for transfers between devices: 6.27 us -> none  [local(): lax.all_to_all(timed.reshape(KPTS, span, 2 * PAIR), 'mom', split_axis=0,...]
    all_to_all x1 -> x0, starting transfers between devices: 4.64 us -> none  [local(): lax.all_to_all(timed.reshape(KPTS, span, 2 * PAIR), 'mom', split_axis=0,...]
    all_to_all x1, waiting for transfers between devices: 42.7 us -> 39.8 us  [local(): lax.all_to_all(pairs, 'shard', split_axis=0, concat_axis=0, tiled=True)]
    pallas_call x1, Pallas kernels: 6.52 us -> 4.78 us  [make_pairs(): pl.pallas_call(pairs_kernel, grid=(LAYERS // STEP_LAYERS,), in_specs=[sme...]
    select_n x0 -> x1, other arithmetic: none -> 1.3 us  [local(): jnp.where(keep, parts, jnp.zeros_like(parts))]
    transpose x1 -> x0, local copies, waits for them, and re-layouts: 1.08 us -> none  [local(): parts = coupling.reshape(NBR, NORB, NORB, PAIR).transpose(1, 0, 2, 3)]
  transfers between devices with their start and end apart: 2 -> 1, of which waited for: 2 -> 1; matrix products, arithmetic and copies ran while one was open for 13% -> 14% of each run, Pallas kernels for 0% -> 0%
where the time goes in v3:
time: 103 us; the launch traced here: 102 us
  waiting for transfers between devices  39.8 us (39%)
  blocking collectives  21.6 us (21%)
  starting transfers between devices  17.8 us (17%)
  local copies, waits for them, and re-layouts  10.7 us (10%)
  Pallas kernels  8.19 us (8%)
  other arithmetic  3.81 us (4%)
    all_to_all x1, waiting for transfers between devices, local(): lax.all_to_all(pairs, 'shard', split_axis=0, concat_axis=0, tiled=True)  39.8 us
    all_to_all x1, starting transfers between devices, local(): lax.all_to_all(pairs, 'shard', split_axis=0, concat_axis=0, tiled=True)  17.8 us
    all_to_all x1, blocking collectives, local(): lax.all_to_all(timed.reshape(KPTS, span, 2 * PAIR), 'mom', split_axis=0,...  11.8 us
    all_to_all x1, blocking collectives, local(): lax.all_to_all(convolved, 'mom', split_axis=0, concat_axis=0, tiled=True)  9.82 us
    mul x4, local copies, waits for them, and re-layouts, local(): terms[..., None] * same  8.5 us
    pallas_call x1, Pallas kernels, make_pairs(): pl.pallas_call(pairs_kernel, grid=(LAYERS // STEP_LAYERS,), in_specs=[sme...  4.78 us
    pallas_call x1, Pallas kernels, local(): pl.pallas_call(couple_kernel, in_specs=[VMEM_SPEC, VMEM_SPEC, pl.BlockSpe...  2.09 us
  transfers between devices with their start and end apart: 1, of which 1 were waited for; matrix products, arithmetic and copies ran while one was open for 14% of the time, Pallas kernels for 0%

profile of v3, /device:TPU:64, one launch (start us, length us, event | category | flops | bytes accessed | tf_op | source)
XLA Modules:
  0.0 102.3 jit_solution(9271204712957426683)
XLA Ops:
  0.0 0.0 copy-start
  0.0 0.0 copy-start.6
  0.0 4.8 %pairs.1 = bf16[64,4,16,128]{3,2,1,0:T(8,128)(2,1)} custom-call(f32[1,4]{1,0:T(1,128)} %occ_ref.1, s32[4,64]{1,0:T(4,128)} %bitcast.55, bf16[1,4,8,2,128,128]{5,4,3,2,1,0:T(8,128)(2,1)} %green_ref.1, bf16[2,128,128]{2,1,0:T(8,128)(2,1)} %broad_ref.1), custom_call_target="tpu_custom_call" | custom-call | tf_op jit(solution)/shard_map/pairs/pallas_call | solution.py:105
  4.8 17.8 %all-to-all-start = ((bf16[64,4,16,128]{3,2,1,0:T(8,128)(2,1)}), bf16[64,4,16,128]{3,2,1,0:T(8,128)(2,1)S(1)}, u32[]{:S(2)}, u32[]{:S(2)}) async-start(bf16[64,4,16,128]{3,2,1,0:T(8,128)(2,1)} %pairs.1), calls=%async_computation | async-start | bytes 2097152 | tf_op jit(solution)/shard_map/all_to_all | solution.py:182
  22.6 0.0 copy-done
  22.6 0.1 constant_dynamic-slice_fusion
  22.7 0.1 reshape.114
  22.7 0.1 dot_general.8
  22.8 0.0 copy-done.6
  22.8 0.2 fusion.5
  23.2 0.3 copy.21
  23.5 2.6 %mul.24 = f32[2,8,2,16,2,8,16]{6,5,4,3,2,1,0:T(8,128)} broadcast(f32[2,8,2,16,2,8]{5,4,3,2,1,0:T(2,128)S(1)} %copy.21), dimensions={0,1,2,3,4,5} | broadcast | bytes 557056 | tf_op jit(solution)/shard_map/mul | solution.py:224
  26.0 4.2 %mul.25 = f32[2,256,256]{2,1,0:T(8,128)} reshape(f32[2,8,2,16,2,8,16]{6,5,4,3,2,1,0:T(8,128)} %mul.24) | data formatting | bytes 1048576 | tf_op jit(solution)/shard_map/mul | solution.py:224
  30.2 0.0 copy-start.5
  30.2 0.0 copy-start.7
  30.3 0.2 mul.26
  30.5 1.5 %mul.27 = f32[256,256]{1,0:T(8,128)} reshape(f32[8,2,16,2,8,16]{5,4,3,2,1,0:T(8,128)S(1)} %mul.26) | data formatting | bytes 524288 | tf_op jit(solution)/shard_map/mul | solution.py:224
  32.0 0.0 copy-done.5
  32.0 0.2 dynamic-slice_reduce_fusion
  32.2 0.0 copy-done.7
  32.2 0.6 dynamic_slice.9
  32.8 0.6 iota_compare_fusion.6
  33.3 0.6 compare_and_fusion
  33.9 0.2 select_reduce_fusion
  34.1 0.1 iota_compare_fusion.5
  34.2 0.1 broadcast_and_fusion
  34.3 1.3 %and_select_fusion = bf16[16,4,16,256]{3,2,0,1:T(8,128)(2,1)S(1)} fusion(bf16[16,4,16,256]{3,2,0,1:T(8,128)(2,1)} %bitcast.53, pred[256]{0:T(512)(128)(4,1)S(1)} %compare_and_fusion, pred[16,4,16]{2,0,1:T(8,128)(4,1)S(1)} %broadcast_and_fusion), kind=kLoop, calls=%fused_computation.5 | loop fusion | flops 524288 | bytes 1049856 | tf_op jit(solution)/shard_map/jit(_where)/select_n | solution.py:198
  35.6 0.0 copy-start.3
  35.6 0.0 copy-start.4
  35.6 0.2 fusion.2
  35.9 0.7 copy-done.3
  36.6 0.1 copy-done.4
  36.7 0.8 subtract_convert_fusion
  37.5 39.8 %all-to-all-done.arrived_ref = bf16[64,4,16,128]{3,2,1,0:T(8,128)(2,1)S(1)} async-done(((bf16[64,4,16,128]{3,2,1,0:T(8,128)(2,1)}), bf16[64,4,16,128]{3,2,1,0:T(8,128)(2,1)S(1)}, u32[]{:S(2)}, u32[]{:S(2)}) %all-to-all-start) | async-done | bytes 1048608 | tf_op jit(solution)/shard_map/all_to_all | solution.py:182
  77.2 0.0 copy-start.1
  77.2 0.0 copy-start.2
  77.2 2.1 %couple.1 = bf16[256,512]{1,0:T(8,128)(2,1)S(1)} custom-call(bf16[64,4,16,128]{3,2,1,0:T(8,128)(2,1)S(1)} %all-to-all-done.arrived_ref, bf16[2048,512]{1,0:T(8,128)(2,1)S(1)} %bitcast.49, bf16[512,256]{1,0:T(8,128)(2,1)} %constant.54.clone.table_hbm), custom_call_target="tpu_custom_call" | custom-call | tf_op jit(solution)/shard_map/couple/pallas_call | solution.py:239
  79.3 11.8 %all_to_all.15.values_ref = bf16[8,32,512]{2,1,0:T(8,128)(2,1)S(1)} all-to-all(bf16[8,32,512]{2,1,0:T(8,128)(2,1)S(1)} %bitcast.50), channel_id=1, replica_groups=mesh['mom'=8,'shard'=64] {'mom'}, dimensions={0} | all-to-all | bytes 524288 | tf_op jit(solution)/shard_map/all_to_all | solution.py:253
  91.1 0.0 copy-done.1
  91.1 0.3 convolve.1
  91.4 9.8 %all_to_all.16 = bf16[8,32,512]{2,1,0:T(8,128)(2,1)S(1)} all-to-all(bf16[8,32,512]{2,1,0:T(8,128)(2,1)S(1)} %convolve.1), channel_id=1, replica_groups=mesh['mom'=8,'shard'=64] {'mom'}, dimensions={0} | all-to-all | bytes 524288 | tf_op jit(solution)/shard_map/all_to_all | solution.py:264
  101.2 0.0 copy-done.2
  101.2 1.0 back.1
  (6 shorter events, 0.1 us)
Async XLA Ops:
  0.0 22.6 %copy-start = (f32[8,2,256]{2,1,0:T(2,128)S(1)}, f32[8,2,256]{2,1,0:T(2,128)}, u32[]{:S(2)}) copy-start(f32[8,2,256]{2,1,0:T(2,128)} %param.16) | copy-start | bytes 49156
  0.0 22.8 %copy-start.6 = (s32[8,8]{1,0:T(8,128)S(1)}, s32[8,8]{1,0:T(8,128)}, u32[]{:S(2)}) copy-start(s32[8,8]{1,0:T(8,128)} %param.17) | copy-start | bytes 772
  4.8 72.5 %all-to-all-start = ((bf16[64,4,16,128]{3,2,1,0:T(8,128)(2,1)}), bf16[64,4,16,128]{3,2,1,0:T(8,128)(2,1)S(1)}, u32[]{:S(2)}, u32[]{:S(2)}) async-start(bf16[64,4,16,128]{3,2,1,0:T(8,128)(2,1)} %pairs.1), calls=%async_computation | async-start | bytes 2097152 | tf_op jit(solution)/shard_map/all_to_all | solution.py:182
  30.2 1.8 %copy-start.5 = (s32[64,4]{0,1:T(4,128)S(1)}, s32[64,4]{0,1:T(4,128)}, u32[]{:S(2)}) copy-start(s32[64,4]{0,1:T(4,128)} %param.13) | copy-start | bytes 3076
  30.2 1.9 %copy-start.7 = (s32[64]{0:T(128)S(1)}, s32[64]{0:T(128)}, u32[]{:S(2)}) copy-start(s32[64]{0:T(128)} %param.14) | copy-start | bytes 772
  35.6 1.0 %copy-start.3 = (f32[2,256,256]{2,1,0:T(8,128)S(1)}, f32[2,256,256]{2,1,0:T(8,128)}, u32[]{:S(2)}) copy-start(f32[2,256,256]{2,1,0:T(8,128)} %mul.25) | copy-start | bytes 1572868
  35.6 1.1 %copy-start.4 = (f32[256,256]{1,0:T(8,128)S(1)}, f32[256,256]{1,0:T(8,128)}, u32[]{:S(2)}) copy-start(f32[256,256]{1,0:T(8,128)} %mul.27) | copy-start | bytes 786436
  77.2 13.9 %copy-start.1 = (bf16[2,256,256]{2,1,0:T(8,128)(2,1)S(1)}, bf16[2,256,256]{2,1,0:T(8,128)(2,1)}, u32[]{:S(2)}) copy-start(bf16[2,256,256]{2,1,0:T(8,128)(2,1)} %get-tuple-element.11.high_ref) | copy-start | bytes 786436
  77.2 24.0 %copy-start.2 = (bf16[512,512]{1,0:T(8,128)(2,1)S(1)}, bf16[512,512]{1,0:T(8,128)(2,1)}, u32[]{:S(2)}) copy-start(bf16[512,512]{1,0:T(8,128)(2,1)} %constant.55.clone.table_ref) | copy-start | bytes 1572868

commit v4 on v3

--- a/solution.py
+++ b/solution.py
@@ -23,9 +23,10 @@
 
 
 def dft_tables(length):
-    counter = np.arange(length)
-    angles = (counter[:, None] * counter[None, :] % length) * (2.0 * np.pi / length)
-    return np.cos(angles).astype(jnp.bfloat16), np.sin(angles).astype(jnp.bfloat16)
+    counter = lax.optimization_barrier(jnp.arange(length, dtype=jnp.int32))
+    phases = counter[:, None] * counter[None, :] % length
+    angles = phases.astype(F32) * (2.0 * np.pi / length)
+    return jnp.cos(angles).astype(BF16), jnp.sin(angles).astype(BF16)
 
 
 def pairs_kernel(occ_ref, nbr_ref, green_ref, broad_ref, out_ref, mix_ref, left_ref, full_ref):
@@ -122,16 +123,13 @@
     )(occupation, neighbours.T, green_ret, broadening)
 
 
-def couple_kernel(arrived_ref, weight_ref, table_hbm, out_ref, wide, table_ref, table_sem):
-    table_copy = pltpu.make_async_copy(table_hbm, table_ref, table_sem)
-    table_copy.start()
+def couple_kernel(arrived_ref, weight_ref, table_ref, out_ref, wide):
     wide[...] = arrived_ref[...].reshape(ENERGIES * NORB, ORB).astype(F32)
     rows = [wide[pl.ds(i, ENERGIES, stride=NORB), :].astype(BF16) for i in range(NORB)]
     total = jnp.dot(
         jnp.concatenate(rows, axis=1), weight_ref[...], preferred_element_type=F32
     )
     coupled = total.astype(BF16)
-    table_copy.wait()
     spectra = jnp.dot(table_ref[...], coupled, preferred_element_type=F32)
     out_ref[:, :PAIR] = (spectra[:ENERGIES, :PAIR] + spectra[ENERGIES:, PAIR:]).astype(BF16)
     out_ref[:, PAIR:] = (spectra[:ENERGIES, PAIR:] - spectra[ENERGIES:, :PAIR]).astype(BF16)
@@ -170,10 +168,6 @@
     return pltpu.with_memory_space_constraint(value, pltpu.VMEM)
 
 
-def in_hbm(value):
-    return pltpu.with_memory_space_constraint(value, pltpu.HBM)
-
-
 def local(
     green_ret, broadening, occupation, neighbours, orbitals, coupling, phonon, mode_table
 ):
@@ -225,30 +219,26 @@
     high = kernels.astype(BF16)
     low = (kernels - high.astype(F32)).astype(BF16)
     cos_table, sin_table = dft_tables(ENERGIES)
-    forward = np.concatenate([cos_table, sin_table], axis=0)
-    wide_cos = cos_table.astype(np.float32)
-    wide_sin = sin_table.astype(np.float32)
-    backward = np.stack(
+    forward = jnp.concatenate([cos_table, sin_table], axis=0)
+    backward = jnp.stack(
         [
-            np.concatenate([wide_cos, -wide_sin], axis=1),
-            np.concatenate([wide_sin, wide_cos], axis=1),
+            jnp.concatenate([cos_table, -sin_table], axis=1),
+            jnp.concatenate([sin_table, cos_table], axis=1),
         ],
         axis=1,
     ).reshape(2 * ENERGIES, 2 * ENERGIES)
-    arrived, weights, high, low = lax.optimization_barrier((arrived, weights, high, low))
+    arrived, weights, high, low, forward, backward = lax.optimization_barrier(
+        (arrived, weights, high, low, forward, backward)
+    )
     timed = pl.pallas_call(
         couple_kernel,
-        in_specs=[VMEM_SPEC, VMEM_SPEC, pl.BlockSpec(memory_space=pltpu.HBM)],
+        in_specs=[VMEM_SPEC] * 3,
         out_specs=VMEM_SPEC,
         out_shape=pltpu.VMEM((ENERGIES, 2 * PAIR), BF16),
-        scratch_shapes=[
-            pltpu.VMEM((ENERGIES * NORB, ORB), F32),
-            pltpu.VMEM((2 * ENERGIES, ENERGIES), BF16),
-            pltpu.SemaphoreType.DMA,
-        ],
+        scratch_shapes=[pltpu.VMEM((ENERGIES * NORB, ORB), F32)],
         compiler_params=pltpu.CompilerParams(vmem_limit_bytes=24 * 2**20),
         name="couple",
-    )(in_vmem(arrived), in_vmem(weights), in_hbm(jnp.asarray(forward)))
+    )(in_vmem(arrived), in_vmem(weights), in_vmem(forward))
 
     moved = lax.all_to_all(
         timed.reshape(KPTS, span, 2 * PAIR), "mom", split_axis=0, concat_axis=0, tiled=True
@@ -270,7 +260,7 @@
         out_shape=jax.ShapeDtypeStruct((1, ENERGIES, 1, 2, PAIR), BF16),
         compiler_params=pltpu.CompilerParams(vmem_limit_bytes=12 * 2**20),
         name="back",
-    )(in_vmem(returned.reshape(ENERGIES, 2 * PAIR)), in_vmem(jnp.asarray(backward, dtype=BF16)))
+    )(in_vmem(returned.reshape(ENERGIES, 2 * PAIR)), in_vmem(backward))
 
 
 def solution(mesh):

time: 103 us -> 102 us (level)
  waiting for transfers between devices: 39.8 us -> 34.3 us
  other arithmetic: 3.81 us -> 7.75 us
  local copies, waits for them, and re-layouts: 10.7 us -> 12.3 us
    all_to_all x1, waiting for transfers between devices: 39.8 us -> 34.3 us  [local(): lax.all_to_all(pairs, 'shard', split_axis=0, concat_axis=0, tiled=True)]
    convert_element_type x0 -> x1, other arithmetic: none -> 1.27 us  [dft_tables(): return (jnp.cos(angles).astype(BF16), jnp.sin(angles).astype(BF16))]
    concatenate x1, other arithmetic: 0.21 us -> 1.47 us  [local(): jnp.concatenate([jnp.concatenate([parts, zeros], axis=2), jnp.concatenate...]
    neg x0 -> x1, other arithmetic: none -> 1.07 us  [local(): -sin_table]
  transfers between devices with their start and end apart: 1 -> 1, of which waited for: 1 -> 1; matrix products, arithmetic and copies ran while one was open for 14% -> 20% of each run, Pallas kernels for 0% -> 0%
where the time goes in v4:
time: 102 us; the launch traced here: 101 us
  waiting for transfers between devices  34.3 us (34%)
  blocking collectives  21.6 us (21%)
  starting transfers between devices  17.8 us (17%)
  local copies, waits for them, and re-layouts  12.3 us (12%)
  other arithmetic  7.75 us (8%)
  Pallas kernels  7.3 us (7%)
    all_to_all x1, waiting for transfers between devices, local(): lax.all_to_all(pairs, 'shard', split_axis=0, concat_axis=0, tiled=True)  34.3 us
    all_to_all x1, starting transfers between devices, local(): lax.all_to_all(pairs, 'shard', split_axis=0, concat_axis=0, tiled=True)  17.8 us
    all_to_all x1, blocking collectives, local(): lax.all_to_all(timed.reshape(KPTS, span, 2 * PAIR), 'mom', split_axis=0,...  11.8 us
    all_to_all x1, blocking collectives, local(): lax.all_to_all(convolved, 'mom', split_axis=0, concat_axis=0, tiled=True)  9.82 us
    mul x4, local copies, waits for them, and re-layouts, local(): terms[..., None] * same  8.51 us
    pallas_call x1, Pallas kernels, make_pairs(): pl.pallas_call(pairs_kernel, grid=(LAYERS // STEP_LAYERS,), in_specs=[sme...  4.78 us
  transfers between devices with their start and end apart: 1, of which 1 were waited for; matrix products, arithmetic and copies ran while one was open for 20% of the time, Pallas kernels for 0%

profile of v4, /device:TPU:64, one launch (start us, length us, event | category | flops | bytes accessed | tf_op | source)
XLA Modules:
  0.0 101.4 jit_solution(8665772915727797691)
XLA Ops:
  0.0 0.0 copy-start
  0.0 0.0 copy-start.7
  0.0 4.8 %pairs.1 = bf16[64,4,16,128]{3,2,1,0:T(8,128)(2,1)} custom-call(f32[1,4]{1,0:T(1,128)} %occ_ref.1, s32[4,64]{1,0:T(4,128)} %bitcast.59, bf16[1,4,8,2,128,128]{5,4,3,2,1,0:T(8,128)(2,1)} %green_ref.1, bf16[2,128,128]{2,1,0:T(8,128)(2,1)} %broad_ref.1), custom_call_target="tpu_custom_call" | custom-call | tf_op jit(solution)/shard_map/pairs/pallas_call | solution.py:106
  4.8 17.8 %all-to-all-start = ((bf16[64,4,16,128]{3,2,1,0:T(8,128)(2,1)}), bf16[64,4,16,128]{3,2,1,0:T(8,128)(2,1)S(1)}, u32[]{:S(2)}, u32[]{:S(2)}) async-start(bf16[64,4,16,128]{3,2,1,0:T(8,128)(2,1)} %pairs.1), calls=%async_computation | async-start | bytes 2097152 | tf_op jit(solution)/shard_map/all_to_all | solution.py:176
  22.6 0.0 copy-done
  22.6 0.1 constant_dynamic-slice_fusion
  22.7 0.1 reshape.119
  22.7 0.1 dot_general.8
  22.8 0.0 copy-done.7
  22.8 0.2 fusion.9
  23.2 0.3 copy.21
  23.5 2.6 %mul.43 = f32[2,8,2,16,2,8,16]{6,5,4,3,2,1,0:T(8,128)} broadcast(f32[2,8,2,16,2,8]{5,4,3,2,1,0:T(2,128)S(1)} %copy.21), dimensions={0,1,2,3,4,5} | broadcast | bytes 557056 | tf_op jit(solution)/shard_map/mul | solution.py:218
  26.0 4.2 %mul.44 = f32[2,256,256]{2,1,0:T(8,128)} reshape(f32[2,8,2,16,2,8,16]{6,5,4,3,2,1,0:T(8,128)} %mul.43) | data formatting | bytes 1048576 | tf_op jit(solution)/shard_map/mul | solution.py:218
  30.3 0.0 copy-start.6
  30.3 0.0 copy-start.8
  30.3 0.2 mul.45
  30.5 1.5 %mul.46 = f32[256,256]{1,0:T(8,128)} reshape(f32[8,2,16,2,8,16]{5,4,3,2,1,0:T(8,128)S(1)} %mul.45) | data formatting | bytes 524288 | tf_op jit(solution)/shard_map/mul | solution.py:218
  32.0 0.0 copy-done.6
  32.0 0.2 dynamic-slice_reduce_fusion
  32.2 0.0 copy-done.8
  32.2 0.6 dynamic_slice.9
  32.8 0.6 iota_compare_fusion.6
  33.5 0.6 compare_and_fusion
  34.1 0.2 select_reduce_fusion
  34.3 0.1 iota_compare_fusion.5
  34.4 0.1 broadcast_and_fusion
  34.4 1.3 %and_select_fusion = bf16[16,4,16,256]{3,2,0,1:T(8,128)(2,1)S(1)} fusion(bf16[16,4,16,256]{3,2,0,1:T(8,128)(2,1)} %bitcast.57, pred[256]{0:T(512)(128)(4,1)S(1)} %compare_and_fusion, pred[16,4,16]{2,0,1:T(8,128)(4,1)S(1)} %broadcast_and_fusion), kind=kLoop, calls=%fused_computation.5 | loop fusion | flops 524288 | bytes 1049856 | tf_op jit(solution)/shard_map/jit(_where)/select_n | solution.py:192
  35.8 0.8 copy.18
  36.6 1.1 %fusion.7 = bf16[256,256]{1,0:T(8,128)(2,1)S(1)} fusion(s32[256]{0:T(256)S(1)} %iota.51), kind=kLoop, calls=%fused_computation.29 | loop fusion | flops 1179648 | bytes 132096 | tf_op jit(solution)/shard_map/neg | solution.py:225
  37.7 1.3 %cosine_convert_fusion = (bf16[256,256]{1,0:T(8,128)(2,1)S(1)}, bf16[256,256]{1,0:T(8,128)(2,1)S(1)}) fusion(s32[256]{0:T(256)S(1)} %iota.51), kind=kLoop, calls=%fused_computation.22 | loop fusion | flops 1048576 | bytes 263168 | tf_op jit(solution)/shard_map/convert_element_type | solution.py:29
  39.0 0.1 pad_maximum_fusion
  39.0 0.5 copy.22
  39.6 1.0 reshape.120.table_ref
  40.6 0.0 copy-start.4
  40.6 0.0 copy-start.5
  40.6 1.5 %fusion.2 = bf16[16,128,512]{2,1,0:T(8,128)(2,1)S(1)} fusion(bf16[16,64,256]{2,1,0:T(8,128)(2,1)} %bitcast.56), kind=kLoop, calls=%fused_computation.4 | loop fusion | flops 8388608 | bytes 2621440 | tf_op jit(solution)/shard_map/concatenate | solution.py:194
  42.1 0.0 copy-done.4
  42.1 0.0 copy-done.5
  42.1 0.9 subtract_convert_fusion
  43.0 34.3 %all-to-all-done.arrived_ref = bf16[64,4,16,128]{3,2,1,0:T(8,128)(2,1)S(1)} async-done(((bf16[64,4,16,128]{3,2,1,0:T(8,128)(2,1)}), bf16[64,4,16,128]{3,2,1,0:T(8,128)(2,1)S(1)}, u32[]{:S(2)}, u32[]{:S(2)}) %all-to-all-start) | async-done | bytes 1048608 | tf_op jit(solution)/shard_map/all_to_all | solution.py:176
  77.3 1.2 %couple.1 = bf16[256,512]{1,0:T(8,128)(2,1)S(1)} custom-call(bf16[64,4,16,128]{3,2,1,0:T(8,128)(2,1)S(1)} %all-to-all-done.arrived_ref, bf16[2048,512]{1,0:T(8,128)(2,1)S(1)} %bitcast.53, bf16[512,256]{1,0:T(8,128)(2,1)S(1)} %pad_maximum_fusion.2.table_ref), custom_call_target="tpu_custom_call" | custom-call | tf_op jit(solution)/shard_map/couple/pallas_call | solution.py:233
  78.5 11.8 %all_to_all.15.values_ref = bf16[8,32,512]{2,1,0:T(8,128)(2,1)S(1)} all-to-all(bf16[8,32,512]{2,1,0:T(8,128)(2,1)S(1)} %bitcast.54), channel_id=1, replica_groups=mesh['mom'=8,'shard'=64] {'mom'}, dimensions={0} | all-to-all | bytes 524288 | tf_op jit(solution)/shard_map/all_to_all | solution.py:243
  90.2 0.0 copy-done.2
  90.2 0.0 copy-done.3
  90.2 0.3 convolve.1
  90.5 9.8 %all_to_all.16 = bf16[8,32,512]{2,1,0:T(8,128)(2,1)S(1)} all-to-all(bf16[8,32,512]{2,1,0:T(8,128)(2,1)S(1)} %convolve.1), channel_id=1, replica_groups=mesh['mom'=8,'shard'=64] {'mom'}, dimensions={0} | all-to-all | bytes 524288 | tf_op jit(solution)/shard_map/all_to_all | solution.py:254
  100.4 0.0 copy-done.1
  100.4 1.0 back.1
  (11 shorter events, 0.1 us)
Async XLA Ops:
  0.0 22.6 %copy-start = (f32[8,2,256]{2,1,0:T(2,128)S(1)}, f32[8,2,256]{2,1,0:T(2,128)}, u32[]{:S(2)}) copy-start(f32[8,2,256]{2,1,0:T(2,128)} %param.14) | copy-start | bytes 49156
  0.0 22.8 %copy-start.7 = (s32[8,8]{1,0:T(8,128)S(1)}, s32[8,8]{1,0:T(8,128)}, u32[]{:S(2)}) copy-start(s32[8,8]{1,0:T(8,128)} %param.15) | copy-start | bytes 772
  4.8 72.5 %all-to-all-start = ((bf16[64,4,16,128]{3,2,1,0:T(8,128)(2,1)}), bf16[64,4,16,128]{3,2,1,0:T(8,128)(2,1)S(1)}, u32[]{:S(2)}, u32[]{:S(2)}) async-start(bf16[64,4,16,128]{3,2,1,0:T(8,128)(2,1)} %pairs.1), calls=%async_computation | async-start | bytes 2097152 | tf_op jit(solution)/shard_map/all_to_all | solution.py:176
  30.3 1.8 %copy-start.6 = (s32[64,4]{0,1:T(4,128)S(1)}, s32[64,4]{0,1:T(4,128)}, u32[]{:S(2)}) copy-start(s32[64,4]{0,1:T(4,128)} %param.11) | copy-start | bytes 3076
  30.3 1.9 %copy-start.8 = (s32[64]{0:T(128)S(1)}, s32[64]{0:T(128)}, u32[]{:S(2)}) copy-start(s32[64]{0:T(128)} %param.12) | copy-start | bytes 772
  40.6 1.5 %copy-start.4 = (f32[2,256,256]{2,1,0:T(8,128)S(1)}, f32[2,256,256]{2,1,0:T(8,128)}, u32[]{:S(2)}) copy-start(f32[2,256,256]{2,1,0:T(8,128)} %mul.44) | copy-start | bytes 1572868
  40.6 1.5 %copy-start.5 = (f32[256,256]{1,0:T(8,128)S(1)}, f32[256,256]{1,0:T(8,128)}, u32[]{:S(2)}) copy-start(f32[256,256]{1,0:T(8,128)} %mul.46) | copy-start | bytes 786436
  77.2 13.0 %copy-start.2 = (bf16[2,256,256]{2,1,0:T(8,128)(2,1)S(1)}, bf16[2,256,256]{2,1,0:T(8,128)(2,1)}, u32[]{:S(2)}) copy-start(bf16[2,256,256]{2,1,0:T(8,128)(2,1)} %get-tuple-element.15.low_ref) | copy-start | bytes 786436
  77.2 13.0 %copy-start.3 = (bf16[2,256,256]{2,1,0:T(8,128)(2,1)S(1)}, bf16[2,256,256]{2,1,0:T(8,128)(2,1)}, u32[]{:S(2)}) copy-start(bf16[2,256,256]{2,1,0:T(8,128)(2,1)} %get-tuple-element.14.high_ref) | copy-start | bytes 786436
  77.2 23.1 %copy-start.1 = (bf16[512,512]{1,0:T(8,128)(2,1)S(1)}, bf16[512,512]{1,0:T(8,128)(2,1)}, u32[]{:S(2)}) copy-start(bf16[512,512]{1,0:T(8,128)(2,1)} %reshape.120.table_ref) | copy-start | bytes 1572868
